TPU v7x, 32 devices: a whole 2x2x4 slice. The times are simulated.
32 devices in a mesh: shot: 2 (over y), gy: 4 (over z), freq: 2 (over x), fld: 2 (over core).
Axes of the slice: x: 2, y: 2, z: 4, core: 2. Of those that a mesh axis runs over, the one named last changes fastest.
Arguments:
- wavefields: float32 [2, 2, 8, 1024, 1024], P('fld', None, ('shot', 'freq'), 'gy'), parts along dimension 2, may hold values from -6 to 6
- slowness: float32 [2, 1024, 1024], P(None, 'gy'), may hold values from 0.7 to 1.3
- freq_index: int32 [4], P('freq'), may hold values from 15 to 27
Outputs:
- image: float32 [4, 1024, 1024], P('shot', 'gy', ('freq', 'fld')), parts along dimension 0
There are 2 independent parts, one for each index of `shot`. A program takes and returns all parts, laid end to end along the dimension named above; an argument that names none is the same for every part. Nothing has to cross between parts.
Inputs may be any that keep to these rules, and one draw needn't show every extreme that they name: `freq_index`: frequency index k stands for the angular frequency 0.1 k.
All inputs are finite; a program needn't handle non-finite values.
Results may differ from a plain program's by a relative error of at most 0.0003.
Values sent between devices are 32-bit elements; how exact they have to be, the bound alone decides.
A program may use at most 64 MiB of HBM per device.

v0:
```python
import math

import jax
import jax.numpy as jnp
from jax import lax
from jax.sharding import PartitionSpec as P

DEPTH = 2


omega_unit = 0.1
reference_slowness = 1.0
depth_interval = 1.0
inner_length = 128


def contract(pattern, values, matrix):
    return jnp.einsum(
        pattern, values, matrix, precision=lax.Precision.HIGHEST, preferred_element_type=jnp.float32
    )


def complex_table(length, polarity):
    indices = jnp.arange(length, dtype=jnp.int32)
    angles = (
        2.0 * math.pi / length * (indices[:, None] * indices[None, :] % length).astype(jnp.float32)
    )
    cosine = jnp.cos(angles)
    sine_part = polarity * jnp.sin(angles)
    upper = jnp.stack([cosine, sine_part], axis=1)
    lower = jnp.stack([-sine_part, cosine], axis=1)
    return jnp.stack([upper, lower], axis=0)


def twiddle(outer_size, inner_size, length, polarity):
    outer_index = jnp.arange(outer_size, dtype=jnp.int32)[:, None]
    inner_index = jnp.arange(inner_size, dtype=jnp.int32)[None, :]
    angles = 2.0 * math.pi / length * (outer_index * inner_index % length).astype(jnp.float32)
    return (jnp.cos(angles), polarity * jnp.sin(angles))


def rotate(values, cosine, sine_part):
    real_part = values[0]
    imag_part = values[1]
    return jnp.stack(
        [real_part * cosine - imag_part * sine_part, real_part * sine_part + imag_part * cosine]
    )


def wave_number(indices, length):
    signed = jnp.where(indices < length // 2, indices, indices - length)
    return 2.0 * math.pi / length * signed.astype(jnp.float32)


def forward_rows(wave_field):
    batches, x_rows, y_cols = wave_field.shape[1:]
    outer_size = y_cols // inner_length
    blocks = wave_field.reshape(2, batches, x_rows, outer_size, inner_length)
    blocks = contract("cbxan,cadk->dbxkn", blocks, complex_table(outer_size, -1.0))
    cosine, sine_part = twiddle(outer_size, inner_length, y_cols, -1.0)
    blocks = rotate(blocks, cosine, sine_part)
    blocks = contract("cbxkn,cndm->dbxkm", blocks, complex_table(inner_length, -1.0))
    return blocks.reshape(2, batches, x_rows, y_cols)


def inverse_rows(wave_field):
    batches, x_rows, y_cols = wave_field.shape[1:]
    outer_size = y_cols // inner_length
    blocks = wave_field.reshape(2, batches, x_rows, outer_size, inner_length)
    blocks = contract("cbxkm,cmdn->dbxkn", blocks, complex_table(inner_length, 1.0))
    cosine, sine_part = twiddle(outer_size, inner_length, y_cols, 1.0)
    blocks = rotate(blocks, cosine, sine_part)
    blocks = contract("cbxkn,ckda->dbxan", blocks, complex_table(outer_size, 1.0))
    return blocks.reshape(2, batches, x_rows, y_cols) / y_cols


def forward_columns(blocks):
    inner_size = blocks.shape[2]
    pencils = blocks.shape[3]
    blocks = contract("cbnsy,csdk->dbnky", blocks, complex_table(pencils, -1.0))
    cosine, sine_part = twiddle(pencils, inner_size, inner_size * pencils, -1.0)
    blocks = rotate(blocks, cosine.T[:, :, None], sine_part.T[:, :, None])
    return contract("cbnky,cndm->dbmky", blocks, complex_table(inner_size, -1.0))


def inverse_columns(blocks):
    inner_size = blocks.shape[2]
    pencils = blocks.shape[3]
    blocks = contract("cbmky,cmdn->dbnky", blocks, complex_table(inner_size, 1.0))
    cosine, sine_part = twiddle(pencils, inner_size, inner_size * pencils, 1.0)
    blocks = rotate(blocks, cosine.T[:, :, None], sine_part.T[:, :, None])
    blocks = contract("cbnky,ckds->dbnsy", blocks, complex_table(pencils, 1.0))
    return blocks / (inner_size * pencils)


def propagate(blocks, omegas, polarities, y_total):
    inner_size, pencils, y_local = blocks.shape[2:]
    x_index = (
        jnp.arange(pencils, dtype=jnp.int32)[None, :]
        + pencils * jnp.arange(inner_size, dtype=jnp.int32)[:, None]
    )
    stored = lax.axis_index("gy") * y_local + jnp.arange(y_local, dtype=jnp.int32)
    y_index = stored // inner_length + y_total // inner_length * (stored % inner_length)
    x_waves = wave_number(x_index, inner_size * pencils)
    y_waves = wave_number(y_index, y_total)
    lateral = x_waves[:, :, None] ** 2 + y_waves[None, None, :] ** 2
    kz_square = ((omegas * reference_slowness) ** 2)[:, None, None, None] - lateral[None]
    kz_root = jnp.sqrt(jnp.abs(kz_square))
    travels = kz_square >= 0.0
    amplitude = jnp.where(travels, 1.0, jnp.exp(-kz_root * depth_interval))
    angles = jnp.where(travels, polarities[:, None, None, None] * kz_root * depth_interval, 0.0)
    return rotate(blocks, amplitude * jnp.cos(angles), amplitude * jnp.sin(angles))


def apply_screen(wave_field, slowness_now, omegas, polarities):
    phases = (polarities * omegas)[:, None, None] * (
        (slowness_now - reference_slowness) * depth_interval
    )[None]
    return rotate(wave_field, jnp.cos(phases), jnp.sin(phases))


def per_device(wavefields, slowness, freq_index):
    x_rows = wavefields.shape[3]
    y_cols = wavefields.shape[4]
    pencils = lax.axis_size("gy")
    freq_devs = lax.axis_size("freq")
    fld_devs = lax.axis_size("fld")
    column_width = y_cols // (freq_devs * fld_devs)
    omegas = omega_unit * freq_index.astype(jnp.float32)
    per_side = wavefields.shape[2] // fld_devs
    regrouped = wavefields.reshape(2, 1, fld_devs, per_side, x_rows, y_cols)
    paired = lax.all_to_all(regrouped, "fld", split_axis=2, concat_axis=1, tiled=True)
    wave_field = paired.reshape(2, fld_devs * per_side, x_rows, y_cols)
    local_omegas = lax.dynamic_slice_in_dim(omegas, lax.axis_index("fld") * per_side, per_side)
    omegas = jnp.tile(local_omegas, fld_devs)
    polarities = jnp.repeat(jnp.array([-1.0, 1.0], jnp.float32), per_side)
    batches = wave_field.shape[1]
    images = []
    for depth_step in range(DEPTH):
        wave_field = forward_rows(wave_field)
        blocks = wave_field.reshape(2, batches, x_rows, pencils, y_cols // pencils)
        blocks = lax.all_to_all(blocks, "gy", split_axis=3, concat_axis=3, tiled=True)
        blocks = forward_columns(blocks)
        blocks = propagate(blocks, omegas, polarities, y_cols)
        blocks = inverse_columns(blocks)
        blocks = lax.all_to_all(blocks, "gy", split_axis=3, concat_axis=3, tiled=True)
        wave_field = inverse_rows(blocks.reshape(2, batches, x_rows, y_cols))
        wave_field = apply_screen(wave_field, slowness[depth_step], omegas, polarities)
        source = wave_field[:, :per_side]
        receiver = wave_field[:, per_side:]
        summed = jnp.sum(source[0] * receiver[0] + source[1] * receiver[1], axis=0)
        partial_image = summed.reshape(x_rows, freq_devs * fld_devs, column_width)[None]
        images.append(
            lax.psum_scatter(partial_image, ("freq", "fld"), scatter_dimension=2, tiled=True)
        )
    combined = jnp.concatenate(images, axis=0)
    return combined.reshape(DEPTH, x_rows, column_width)


def solution(mesh):
    placed = (P("fld", None, ("shot", "freq"), "gy", None), P(None, "gy", None), P("freq"))
    return jax.shard_map(
        per_device,
        mesh=mesh,
        in_specs=placed,
        out_specs=P("shot", "gy", ("freq", "fld")),
        check_vma=False,
    )
```

profile of v0, /device:TPU:0, one launch (start us, length us, event | category | flops | bytes accessed | tf_op | source)
XLA Modules:
  0.0 677.2 jit_solution(15536558963621516833)
XLA Ops:
  11.3 5.6 all-to-all-start
  29.8 5.3 fusion.29
  35.1 7.3 %copy.203 = f32[2,2,256,4,256]{4,0,2,1,3:T(2,128)} copy(f32[2,2,256,4,256]{2,4,3,1,0:T(8,128)} %bitcast.290) | data formatting | bytes 8388608 | tf_op jit(solution)/shard_map/reshape;reshape | solution.py:141
  42.4 6.6 all-to-all-start.1
  60.9 81.8 %all-to-all-done.1 = f32[2,2,256,4,256]{4,0,2,1,3:T(2,128)} async-done(((f32[2,2,256,4,256]{4,0,2,1,3:T(2,128)}), f32[2,2,256,4,256]{4,0,2,1,3:T(2,128)}, u32[]{:S(2)}, u32[]{:S(2)}) %all-to-all-start.1) | async-done | bytes 4194336 | tf_op jit(solution)/shard_map/all_to_all | solution.py:142
  142.7 14.5 %fusion.57 = f32[2,2,256,4,256]{4,3,2,1,0:T(4,128)S(1)} fusion(f32[2,2,256,4,256]{4,0,2,1,3:T(2,128)} %all-to-all-done.1, f32[1,4,2,4]{1,3,0,2:T(4,128)} %copy.196, f32[1,4,2,4]{1,3,0,2:T(4,128)} %copy.195), kind=kOutput, calls=%fused_computation.79 | convolution fusion | flops 100663360 | bytes 8388864 | tf_op jit(solution)/shard_map/cbnsy,csdk->dbnky/dot_general | solution.py:18
  160.0 7.3 %fusion.72 = f32[2,2,256,4,256]{4,2,3,1,0:T(8,128)S(1)} fusion(f32[2,2,256,4,256]{4,3,2,1,0:T(4,128)S(1)} %pad_maximum_fusion.1, f32[1,256,2,256]{1,3,0,2:T(8,128)S(1)} %copy-done.6, f32[1,256,2,256]{1,3,0,2:T(8,128)S(1)} %copy-done.8), kind=kOutput, calls=%fused_computation.84 | convolution fusion | flops 6442713088 | bytes 9437184 | tf_op jit(solution)/shard_map/cbnky,cndm->dbmky/dot_general | solution.py:18
  167.3 8.5 %multiply_subtract_fusion.7 = (f32[1,2,256,4,256]{4,2,3,1,0:T(8,128)S(1)}, f32[1,2,256,4,256]{4,2,3,1,0:T(8,128)S(1)}) fusion(f32[2,2,256,4,256]{4,2,3,1,0:T(8,128)S(1)} %fusion.72, f32[256,4,256]{2,0,1:T(8,128)S(1)} %get-tuple-element.44, f32[2]{0:T(128)S(1)} %copy-done.37, f32[256,4,256]{2,0,1:T(8,128)S(1)} %get-tuple-element.43, ...), kind=kLoop, calls=%fused_computation.107 | loop fusion | flops 5767168 | bytes 10747912 | tf_op jit(solution)/shard_map/sub | solution.py:46
  175.8 7.2 %fusion.75 = f32[2,256,2,4,256]{4,1,3,2,0:T(8,128)S(1)} fusion(f32[1,2,256,4,256]{4,2,3,1,0:T(8,128)S(1)} %get-tuple-element.8, f32[1,2,256,4,256]{4,2,3,1,0:T(8,128)S(1)} %get-tuple-element.7, f32[1,256,2,256]{1,3,2,0:T(8,128)S(1)} %get-tuple-element.38, f32[1,256,2,256]{1,3,2,0:T(8,128)S(1)} %get-tuple-element.35), kind=kOutput, calls=%fused_computation.85 | convolution fusion | flops 6443761664 | bytes 9437184 | tf_op jit(solution)/shard_map/cbmky,cmdn->dbnky/dot_general | solution.py:18
  186.9 9.5 %fusion.20 = f32[2,2,256,4,256]{4,3,2,1,0:T(4,128)S(1)} fusion(f32[1,4,2,4]{1,3,0,2:T(4,128)S(1)} %copy-done.35, f32[1,4,2,4]{1,3,0,2:T(4,128)S(1)} %copy-done.33, f32[1,2,256,4,256]{4,3,2,1,0:T(4,128)S(1)} %get-tuple-element.18, f32[1,2,256,4,256]{4,3,2,1,0:T(4,128)S(1)} %get-tuple-element.17), kind=kOutput, calls=%fused_computation.35 | convolution fusion | flops 102760512 | bytes 8388864 | tf_op jit(solution)/shard_map/cbnky,ckds->dbnsy/dot_general | solution.py:18
  199.2 5.4 all-to-all-start.2
  210.2 87.2 %all-to-all-done.2 = f32[2,2,256,4,256]{4,2,1,0,3:T(8,128)} async-done(((f32[2,2,256,4,256]{4,2,1,0,3:T(8,128)}), f32[2,2,256,4,256]{4,2,1,0,3:T(8,128)}, u32[]{:S(2)}, u32[]{:S(2)}) %all-to-all-start.2) | async-done | bytes 4194336 | tf_op jit(solution)/shard_map/all_to_all | solution.py:146
  297.5 5.3 copy.214
  302.8 5.6 copy.259
  308.4 5.3 convolution_bitcast_fusion.1
  324.2 10.6 %fusion.86 = (f32[1,2,256,1024]{2,3,1,0:T(8,128)S(1)}, f32[1,2,256,1024]{2,3,1,0:T(8,128)}) fusion(f32[1,2,256,8,128]{2,4,3,1,0:T(8,128)} %copy.292, f32[1,2,256,8,128]{2,4,3,1,0:T(8,128)} %copy.291, f32[256,1024]{0,1:T(8,128)} %copy.219, f32[2]{0:T(128)} %broadcast_multiply_fusion.6), kind=kLoop, calls=%fused_computation.90 | loop fusion | flops 3670016 | bytes 9437192 | tf_op jit(solution)/shard_map/sub | solution.py:46
  339.6 5.5 fusion.71
  346.5 5.2 fusion.15
  351.7 7.3 %copy.227 = f32[2,2,256,4,256]{4,0,2,1,3:T(2,128)} copy(f32[2,2,256,4,256]{2,4,3,1,0:T(8,128)} %bitcast.288) | data formatting | bytes 8388608 | tf_op jit(solution)/shard_map/reshape;reshape | solution.py:141
  359.0 96.6 %all_to_all.29 = f32[2,2,256,4,256]{4,0,2,1,3:T(2,128)S(1)} all-to-all(f32[2,2,256,4,256]{4,0,2,1,3:T(2,128)} %copy.227), channel_id=1, replica_groups=mesh['shot'=2,'gy'=4,'freq'=2,'fld'=2] {'gy'}, dimensions={3} | all-to-all | bytes 8388608 | tf_op jit(solution)/shard_map/all_to_all | solution.py:142
  455.6 10.3 %fusion.64 = f32[2,2,256,4,256]{4,3,2,1,0:T(4,128)S(1)} fusion(f32[2,2,256,4,256]{4,0,2,1,3:T(2,128)S(1)} %all_to_all.29, f32[1,4,2,4]{1,3,0,2:T(4,128)S(1)} %copy-done.28, f32[1,4,2,4]{1,3,0,2:T(4,128)S(1)} %copy-done.27), kind=kOutput, calls=%fused_computation.80 | convolution fusion | flops 100663360 | bytes 8388864 | tf_op jit(solution)/shard_map/cbnsy,csdk->dbnky/dot_general | solution.py:18
  468.4 7.3 %fusion.78 = f32[2,2,256,4,256]{4,2,3,1,0:T(8,128)S(1)} fusion(f32[2,2,256,4,256]{4,3,2,1,0:T(4,128)S(1)} %pad_maximum_fusion.6, f32[1,256,2,256]{1,3,0,2:T(8,128)S(1)} %copy-done.7, f32[1,256,2,256]{1,3,0,2:T(8,128)S(1)} %copy-done.9), kind=kOutput, calls=%fused_computation.86 | convolution fusion | flops 6442713088 | bytes 9437184 | tf_op jit(solution)/shard_map/cbnky,cndm->dbmky/dot_general | solution.py:18
  475.8 8.7 %multiply_subtract_fusion.2 = (f32[1,2,256,4,256]{4,2,3,1,0:T(8,128)S(1)}, f32[1,2,256,4,256]{4,2,3,1,0:T(8,128)S(1)}) fusion(f32[2,2,256,4,256]{4,2,3,1,0:T(8,128)S(1)} %fusion.78, f32[256,4,256]{2,0,1:T(8,128)S(1)} %copy-done.1, f32[2]{0:T(128)S(1)} %copy-done.39, f32[256,4,256]{2,0,1:T(8,128)S(1)} %get-tuple-element.43, pred[256,4,256]{2,0,1:T(8,128)(4,1)S(1)} %fusion.90), kind=kLoop, calls=%fused_computation.97 | loop fusion | flops 5767168 | bytes 10747912 | tf_op jit(solution)/shard_map/sub | solution.py:46
  484.5 7.2 %fusion.81 = f32[2,256,2,4,256]{4,1,3,2,0:T(8,128)S(1)} fusion(f32[1,2,256,4,256]{4,2,3,1,0:T(8,128)S(1)} %get-tuple-element.6, f32[1,2,256,4,256]{4,2,3,1,0:T(8,128)S(1)} %get-tuple-element.5, f32[1,256,2,256]{1,3,2,0:T(8,128)S(1)} %copy-done.5, f32[1,256,2,256]{1,3,2,0:T(8,128)S(1)} %copy-done.3), kind=kOutput, calls=%fused_computation.87 | convolution fusion | flops 6443761664 | bytes 9437184 | tf_op jit(solution)/shard_map/cbmky,cmdn->dbnky/dot_general | solution.py:18
  495.6 9.7 %fusion.6 = f32[2,2,256,4,256]{4,3,2,1,0:T(4,128)S(1)} fusion(f32[1,4,2,4]{1,3,0,2:T(4,128)S(1)} %copy-done.36, f32[1,4,2,4]{1,3,0,2:T(4,128)S(1)} %copy-done.34, f32[1,2,256,4,256]{4,3,2,1,0:T(4,128)S(1)} %get-tuple-element.14, f32[1,2,256,4,256]{4,3,2,1,0:T(4,128)S(1)} %get-tuple-element.13), kind=kOutput, calls=%fused_computation.19 | convolution fusion | flops 102760512 | bytes 8388864 | tf_op jit(solution)/shard_map/cbnky,ckds->dbnsy/dot_general | solution.py:18
  508.1 4.9 all-to-all-start.4
  517.4 87.7 %all-to-all-done.4 = f32[2,2,256,4,256]{4,2,1,0,3:T(8,128)} async-done(((f32[2,2,256,4,256]{4,2,1,0,3:T(8,128)}), f32[2,2,256,4,256]{4,2,1,0,3:T(8,128)}, u32[]{:S(2)}, u32[]{:S(2)}) %all-to-all-start.4) | async-done | bytes 4194336 | tf_op jit(solution)/shard_map/all_to_all | solution.py:146
  605.1 5.5 copy.235
  610.7 5.6 copy.271
  616.3 5.3 convolution_bitcast_fusion
  633.2 9.5 %fusion.84 = (f32[1,2,256,1024]{2,3,1,0:T(8,128)S(1)}, f32[1,2,256,1024]{2,3,1,0:T(8,128)S(1)}) fusion(f32[1,2,256,8,128]{2,4,3,1,0:T(8,128)} %copy.294, f32[1,2,256,8,128]{2,4,3,1,0:T(8,128)S(1)} %copy.293, f32[256,1024]{0,1:T(8,128)S(1)} %copy.240, f32[2]{0:T(128)S(1)} %copy-done.40), kind=kLoop, calls=%fused_computation.88 | loop fusion | flops 3670016 | bytes 9437192 | tf_op jit(solution)/shard_map/sub | solution.py:46
  644.0 24.0 %reduce-scatter.5.cloned.1.call-done = f32[1,256,1,256]{1,3,2,0:T(8,128)} async-done(((f32[1,256,4,256]{1,3,2,0:T(8,128)}), f32[1,256,1,256]{1,3,2,0:T(8,128)}) %reduce-scatter.5.cloned.1.call-update) | async-done | bytes 262160 | tf_op jit(solution)/shard_map/reduce_scatter | solution.py:154
  (166 shorter events, 88.3 us)
Async XLA Ops:
  11.3 10.1 %all-to-all-start = ((f32[2,1,2,1,256,1024]{5,4,0,3,1,2:T(8,128)}), f32[2,1,2,1,256,1024]{5,4,0,3,1,2:T(8,128)}, u32[]{:S(2)}, u32[]{:S(2)}) async-start(f32[2,1,2,1,256,1024]{5,4,0,3,1,2:T(8,128)} %bitcast.285), calls=%async_computation | async-start | bytes 8388608 | tf_op jit(solution)/shard_map/all_to_all | solution.py:132
  18.7 5.9 copy-start.22
  29.8 5.3 copy-start.18
  29.8 5.3 copy-start.20
  42.4 9.3 %copy-start.41 = (s32[2]{0:T(128)S(1)}, s32[2]{0:T(128)}, u32[]{:S(2)}) copy-start(s32[2]{0:T(128)} %param.6) | copy-start | bytes 28
  42.4 100.4 %all-to-all-start.1 = ((f32[2,2,256,4,256]{4,0,2,1,3:T(2,128)}), f32[2,2,256,4,256]{4,0,2,1,3:T(2,128)}, u32[]{:S(2)}, u32[]{:S(2)}) async-start(f32[2,2,256,4,256]{4,0,2,1,3:T(2,128)} %copy.203), calls=%async_computation.1 | async-start | bytes 8388608 | tf_op jit(solution)/shard_map/all_to_all | solution.py:142
  60.1 115.7 %copy-start.2 = (f32[1,256,2,256]{1,3,2,0:T(8,128)}, f32[1,256,2,256]{1,3,2,0:T(8,128)S(1)}, u32[]{:S(2)}) copy-start(f32[1,256,2,256]{1,3,2,0:T(8,128)S(1)} %get-tuple-element.35) | copy-start | bytes 1572868
  60.1 115.7 %copy-start.4 = (f32[1,256,2,256]{1,3,2,0:T(8,128)}, f32[1,256,2,256]{1,3,2,0:T(8,128)S(1)}, u32[]{:S(2)}) copy-start(f32[1,256,2,256]{1,3,2,0:T(8,128)S(1)} %get-tuple-element.38) | copy-start | bytes 1572868
  60.9 106.4 %copy-start = (f32[256,4,256]{2,0,1:T(8,128)}, f32[256,4,256]{2,0,1:T(8,128)S(1)}, u32[]{:S(2)}) copy-start(f32[256,4,256]{2,0,1:T(8,128)S(1)} %get-tuple-element.44) | copy-start | bytes 3145732
  142.7 14.5 %copy-start.12 = (f32[256,4]{1,0:T(8,128)S(1)}, f32[256,4]{1,0:T(8,128)}, u32[]{:S(2)}) copy-start(f32[256,4]{1,0:T(8,128)} %copy.206) | copy-start | bytes 12292
  160.0 7.3 %copy-start.37 = (f32[2]{0:T(128)S(1)}, f32[2]{0:T(128)}, u32[]{:S(2)}) copy-start(f32[2]{0:T(128)} %constant.219.clone) | copy-start | bytes 28
  199.2 5.4 copy-start.32
  199.2 5.5 copy-start.31
  199.2 98.3 %all-to-all-start.2 = ((f32[2,2,256,4,256]{4,2,1,0,3:T(8,128)}), f32[2,2,256,4,256]{4,2,1,0,3:T(8,128)}, u32[]{:S(2)}, u32[]{:S(2)}) async-start(f32[2,2,256,4,256]{4,2,1,0,3:T(8,128)} %copy.213), calls=%async_computation.2 | async-start | bytes 8388608 | tf_op jit(solution)/shard_map/all_to_all | solution.py:146
  204.7 109.4 %copy-start.23 = (f32[1,8,2,8]{1,3,0,2:T(8,128)}, f32[1,8,2,8]{1,3,0,2:T(8,128)S(1)}, u32[]{:S(2)}) copy-start(f32[1,8,2,8]{1,3,0,2:T(8,128)S(1)} %copy.190) | copy-start | bytes 1540
  204.8 109.4 %copy-start.25 = (f32[1,8,2,8]{1,3,0,2:T(8,128)}, f32[1,8,2,8]{1,3,0,2:T(8,128)S(1)}, u32[]{:S(2)}) copy-start(f32[1,8,2,8]{1,3,0,2:T(8,128)S(1)} %copy.191) | copy-start | bytes 1540
  209.0 104.7 %copy-start.29 = (f32[8,128]{1,0:T(8,128)}, f32[8,128]{1,0:T(8,128)S(1)}, u32[]{:S(2)}) copy-start(f32[8,128]{1,0:T(8,128)S(1)} %fusion.154) | copy-start | bytes 12292
  302.8 5.6 copy-start.14
  302.8 5.6 copy-start.16
  359.0 96.6 %copy-start.27 = (f32[1,4,2,4]{1,3,0,2:T(4,128)S(1)}, f32[1,4,2,4]{1,3,0,2:T(4,128)}, u32[]{:S(2)}) copy-start(f32[1,4,2,4]{1,3,0,2:T(4,128)} %copy.195) | copy-start | bytes 388
  359.0 96.6 %copy-start.28 = (f32[1,4,2,4]{1,3,0,2:T(4,128)S(1)}, f32[1,4,2,4]{1,3,0,2:T(4,128)}, u32[]{:S(2)}) copy-start(f32[1,4,2,4]{1,3,0,2:T(4,128)} %copy.196) | copy-start | bytes 388
  455.6 10.3 %copy-start.13 = (f32[256,4]{1,0:T(8,128)S(1)}, f32[256,4]{1,0:T(8,128)}, u32[]{:S(2)}) copy-start(f32[256,4]{1,0:T(8,128)} %copy.206) | copy-start | bytes 12292
  468.4 7.3 %copy-start.1 = (f32[256,4,256]{2,0,1:T(8,128)S(1)}, f32[256,4,256]{2,0,1:T(8,128)}, u32[]{:S(2)}) copy-start(f32[256,4,256]{2,0,1:T(8,128)} %copy-done) | copy-start | bytes 3145732
  468.4 7.3 %copy-start.39 = (f32[2]{0:T(128)S(1)}, f32[2]{0:T(128)}, u32[]{:S(2)}) copy-start(f32[2]{0:T(128)} %constant.219.clone) | copy-start | bytes 28
  475.8 8.7 %copy-start.3 = (f32[1,256,2,256]{1,3,2,0:T(8,128)S(1)}, f32[1,256,2,256]{1,3,2,0:T(8,128)}, u32[]{:S(2)}) copy-start(f32[1,256,2,256]{1,3,2,0:T(8,128)} %copy-done.2) | copy-start | bytes 1572868
  475.8 8.7 %copy-start.5 = (f32[1,256,2,256]{1,3,2,0:T(8,128)S(1)}, f32[1,256,2,256]{1,3,2,0:T(8,128)}, u32[]{:S(2)}) copy-start(f32[1,256,2,256]{1,3,2,0:T(8,128)} %copy-done.4) | copy-start | bytes 1572868
  508.1 97.1 %all-to-all-start.4 = ((f32[2,2,256,4,256]{4,2,1,0,3:T(8,128)}), f32[2,2,256,4,256]{4,2,1,0,3:T(8,128)}, u32[]{:S(2)}, u32[]{:S(2)}) async-start(f32[2,2,256,4,256]{4,2,1,0,3:T(8,128)} %copy.234), calls=%async_computation.5 | async-start | bytes 8388608 | tf_op jit(solution)/shard_map/all_to_all | solution.py:146
  512.9 131.1 %reduce-scatter.3.cloned.1.call-start = ((), (), s32[]{:S(2)}) async-start(), calls=%async_computation.7 | async-start | bytes 1310720 | tf_op jit(solution)/shard_map/reduce_scatter | solution.py:154
  517.4 150.7 %reduce-scatter.5.cloned.1.call-start = ((), (), s32[]{:S(2)}) async-start(), calls=%async_computation.8 | async-start | bytes 1310720 | tf_op jit(solution)/shard_map/reduce_scatter | solution.py:154
  610.7 5.6 copy-start.15
  610.7 5.6 copy-start.17
  616.2 5.3 copy-start.30
  (16 other events, 22.1 us)
Sparse Core Ops, SparseCore 0:
  517.5 26.2 reduce-scatter.2
  644.1 23.9 reduce-scatter.4
where the time goes:
time: 686 us; the launch traced here: 677 us
  waiting for transfers between devices  284 us (41%)
  matrix products  111 us (16%)
  blocking collectives  96.6 us (14%)
  local copies, waits for them, and re-layouts  84.5 us (12%)
  other arithmetic  63.5 us (9%)
  starting transfers between devices  22.5 us (3%)
  between operations  15.8 us (2%)
    all_to_all x3, waiting for transfers between devices, per_device(): lax.all_to_all(blocks, 'gy', split_axis=3, concat_axis=3, tiled=True)  257 us
    dot_general x16, matrix products, contract(): jnp.einsum(pattern, values, matrix, precision=lax.Precision.HIGHEST, pref...  111 us
    all_to_all x1, blocking collectives, per_device(): lax.all_to_all(blocks, 'gy', split_axis=3, concat_axis=3, tiled=True)  96.6 us
    sub x12, other arithmetic, rotate(): real_part * cosine - imag_part * sine_part  44 us
    reduce_scatter x2, waiting for transfers between devices, per_device(): lax.psum_scatter(partial_image, ('freq', 'fld'), scatter_dimension=2, til...  24.1 us
    all_to_all x3, starting transfers between devices, per_device(): lax.all_to_all(blocks, 'gy', split_axis=3, concat_axis=3, tiled=True)  16.9 us
    another operation x2, local copies, waits for them, and re-layouts, per_device(): blocks = wave_field.reshape(2, batches, x_rows, pencils, y_cols // pencils)  14.5 us
  transfers between devices with their start and end apart: 6, of which 5 were waited for; matrix products, arithmetic and copies ran while one was open for 9% of the time, Pallas kernels for 0%

commit v1 on v0

--- a/solution.py
+++ b/solution.py
@@ -1,8 +1,12 @@
+import functools
 import math
 
 import jax
 import jax.numpy as jnp
+import numpy as np
 from jax import lax
+from jax.experimental import pallas as pl
+from jax.experimental.pallas import tpu as pltpu
 from jax.sharding import PartitionSpec as P
 
 DEPTH = 2
@@ -157,12 +161,369 @@
     return combined.reshape(DEPTH, x_rows, column_width)
 
 
+radix = 4
+MESH = pl.DeviceIdType.MESH
+
+
+def split_table(length):
+    index = np.arange(length)
+    angles = 2.0 * np.pi / length * (index[:, None] * index[None, :] % length)
+    cosine, sine = np.cos(angles), np.sin(angles)
+    right = np.block([[cosine, -sine], [sine, cosine]]).astype(np.float32)
+    high = right.astype(jnp.bfloat16)
+    low = (right - high.astype(np.float32)).astype(jnp.bfloat16)
+    return np.stack([high, low]), np.stack([high.T, low.T])
+
+
+def twiddle_angles(length):
+    short = length // radix
+    return 2.0 * np.pi / length * (np.arange(radix)[:, None] * np.arange(short)[None, :])
+
+
+def halves(values):
+    high = values.astype(jnp.bfloat16)
+    return high, (values - high.astype(jnp.float32)).astype(jnp.bfloat16)
+
+
+def dot32(left, right):
+    return jnp.dot(left, right, preferred_element_type=jnp.float32)
+
+
+def times_table(values, table):
+    high, low = halves(values)
+    return dot32(high, table[0]) + (dot32(low, table[0]) + dot32(high, table[1]))
+
+
+def table_times(table, values):
+    high, low = halves(values)
+    return dot32(table[0], high) + (dot32(table[0], low) + dot32(table[1], high))
+
+
+def butterfly(parts, sign):
+    (r0, i0), (r1, i1), (r2, i2), (r3, i3) = parts
+    ar, ai, br, bi = r0 + r2, i0 + i2, r0 - r2, i0 - i2
+    cr, ci, dr, di = r1 + r3, i1 + i3, r1 - r3, i1 - i3
+    er, ei = -sign * di, sign * dr
+    return [(ar + cr, ai + ci), (br + er, bi + ei), (ar - cr, ai - ci), (br - er, bi - ei)]
+
+
+def turn(part, cosine, sine):
+    return part[0] * cosine - part[1] * sine, part[0] * sine + part[1] * cosine
+
+
+def rows_forward(parts, table, twiddles):
+    rows, short = parts[0][0].shape
+    parts = butterfly(parts, -1.0)
+    parts = [parts[0]] + [turn(parts[k], twiddles[0, k:k + 1], -twiddles[1, k:k + 1]) for k in range(1, radix)]
+    stacked = jnp.concatenate([jnp.concatenate(part, axis=1) for part in parts], axis=0)
+    spectra = times_table(stacked, table)
+    return [(spectra[k * rows:(k + 1) * rows, :short], spectra[k * rows:(k + 1) * rows, short:]) for k in range(radix)]
+
+
+def rows_inverse(parts, table, twiddles):
+    rows, short = parts[0][0].shape
+    stacked = jnp.concatenate([jnp.concatenate(part, axis=1) for part in parts], axis=0)
+    fields = times_table(stacked, table)
+    parts = [(fields[k * rows:(k + 1) * rows, :short], fields[k * rows:(k + 1) * rows, short:]) for k in range(radix)]
+    parts = [parts[0]] + [turn(parts[k], twiddles[0, k:k + 1], twiddles[1, k:k + 1]) for k in range(1, radix)]
+    return butterfly(parts, 1.0)
+
+
+def small_sincos(angle):
+    square = angle * angle
+    sine = 1.0
+    for n in (14, 12, 10, 8, 6, 4, 2):
+        sine = 1.0 - square * (1.0 / (n * (n + 1))) * sine
+    cosine = 1.0
+    for n in (13, 11, 9, 7, 5, 3, 1):
+        cosine = 1.0 - square * (1.0 / (n * (n + 1))) * cosine
+    return angle * sine, cosine
+
+
+def spread_kernel(axes, x_total, y_total, step_rows, fields_ref, scalars_ref, out_ref, prop_ref, send_sem, recv_sem, self_sem):
+    gy, fld = axes
+    me, core = lax.axis_index("gy"), lax.axis_index("fld")
+    freqs = fields_ref.shape[2]
+    half = out_ref.shape[2]
+    barrier = pltpu.get_barrier_semaphore()
+    for dz in range(gy):
+        for dc in range(fld):
+            if dz + dc > 0:
+                pl.semaphore_signal(
+                    barrier, inc=1, device_id_type=MESH,
+                    device_id={"gy": lax.rem(me + dz, gy), "fld": lax.rem(core + dc, fld)},
+                )
+    pl.semaphore_wait(barrier, gy * fld - 1)
+
+    def remote(f, h):
+        return pltpu.make_async_remote_copy(
+            src_ref=fields_ref.at[0, :, f, pl.ds(h * half, half), :],
+            dst_ref=out_ref.at[me],
+            send_sem=send_sem.at[f * fld + h],
+            recv_sem=recv_sem.at[me],
+            device_id={"gy": f * fld + core, "fld": h},
+            device_id_type=MESH,
+        )
+
+    own_f, own_h = me // fld, core
+    is_mine = lax.rem(me, fld) == core
+    own = pltpu.make_async_copy(
+        fields_ref.at[0, :, own_f, pl.ds(pl.multiple_of(own_h * half, half), half), :], out_ref.at[me], self_sem
+    )
+    order = [(f, h) for f in range(freqs) for h in range(fld)]
+    for f, h in order:
+        mine = jnp.logical_and(f * fld + core == me, core == h)
+
+        @pl.when(jnp.logical_not(mine))
+        def _(f=f, h=h):
+            remote(f, h).start()
+
+    @pl.when(is_mine)
+    def _():
+        own.start()
+
+    omega, polarity = scalars_ref[0], scalars_ref[1]
+    x_short, y_short = x_total // radix, y_total // radix
+    width = prop_ref.shape[2]
+
+    @pl.loop(0, x_total // step_rows)
+    def _(step):
+        start = pl.multiple_of(step * step_rows, step_rows)
+        stored_x = start + lax.broadcasted_iota(jnp.int32, (step_rows, width), 0)
+        stored_y = core * width + lax.broadcasted_iota(jnp.int32, (step_rows, width), 1)
+        x_index = stored_x // x_short + radix * (stored_x % x_short)
+        y_index = stored_y // y_short + radix * (stored_y % y_short)
+        lateral = wave_number(x_index, x_total) ** 2 + wave_number(y_index, y_total) ** 2
+        kz_square = (omega * reference_slowness) ** 2 - lateral
+        kz_root = jnp.sqrt(jnp.abs(kz_square))
+        travels = kz_square >= 0.0
+        amplitude = jnp.where(travels, 1.0, jnp.exp(-kz_root * depth_interval)) * (1.0 / (x_total * y_total))
+        sine, cosine = small_sincos(jnp.where(travels, 0.5 * polarity * kz_root * depth_interval, 0.0))
+        prop_ref[0, pl.ds(start, step_rows), :] = amplitude * (1.0 - 2.0 * sine * sine)
+        prop_ref[1, pl.ds(start, step_rows), :] = amplitude * (2.0 * sine * cosine)
+
+    for f, h in order:
+        mine = jnp.logical_and(f * fld + core == me, core == h)
+
+        @pl.when(jnp.logical_not(mine))
+        def _(f=f, h=h):
+            remote(f, h).wait_send()
+
+    for source in range(gy):
+        mine = jnp.logical_and(is_mine, me == source)
+
+        @pl.when(jnp.logical_not(mine))
+        def _(source=source):
+            pltpu.make_async_remote_copy(
+                src_ref=out_ref.at[source], dst_ref=out_ref.at[source],
+                send_sem=send_sem.at[0], recv_sem=recv_sem.at[source],
+                device_id={"gy": me, "fld": 1 - core}, device_id_type=MESH,
+            ).wait_recv()
+
+    @pl.when(is_mine)
+    def _():
+        own.wait()
+
+
+def spread(fields, scalars, gy, fld, x_total, y_total):
+    half = fields.shape[3] // fld
+    width = y_total // fld
+    return pl.pallas_call(
+        functools.partial(spread_kernel, (gy, fld), x_total, y_total, 16),
+        name="spread",
+        out_shape=(
+            jax.ShapeDtypeStruct((gy, 2, half, y_total), jnp.float32),
+            jax.ShapeDtypeStruct((2, x_total, width), jnp.float32),
+        ),
+        in_specs=[pl.BlockSpec(memory_space=pl.ANY), pl.BlockSpec(memory_space=pltpu.SMEM)],
+        out_specs=(pl.BlockSpec(memory_space=pl.ANY), pl.BlockSpec(memory_space=pltpu.VMEM)),
+        scratch_shapes=[
+            pltpu.SemaphoreType.DMA((fields.shape[2] * fld,)),
+            pltpu.SemaphoreType.DMA((gy,)),
+            pltpu.SemaphoreType.DMA,
+        ],
+        compiler_params=pltpu.CompilerParams(collective_id=0, has_side_effects=True, vmem_limit_bytes=16 * 2**20),
+        cost_estimate=pl.CostEstimate(flops=10**8, bytes_accessed=3 * 10**8, transcendentals=10**6),
+    )(fields, scalars)
+
+
+def write_spectrum(out_ref, spectra):
+    per_core = radix // out_ref.shape[0]
+    short = spectra[0][0].shape[1]
+    for k in range(radix):
+        lanes = pl.ds(k % per_core * short, short)
+        for part in range(2):
+            out_ref[k // per_core, 0, part, :, lanes] = spectra[k][part]
+
+
+def lane_parts(ref, index, short):
+    return [
+        tuple(ref[index + (part, slice(None), pl.ds(n * short, short))] for part in range(2)) for n in range(radix)
+    ]
+
+
+def first_kernel(field_ref, table_ref, twiddle_ref, out_ref):
+    short = twiddle_ref.shape[2]
+    write_spectrum(out_ref, rows_forward(lane_parts(field_ref, (0,), short), table_ref, twiddle_ref[...]))
+
+
+def middle_kernel(blocks_ref, prop_ref, table_ref, back_ref, twiddle_ref, out_ref):
+    cores, chunks, _, half, cols = blocks_ref.shape
+    short = cores * half
+    parts = [
+        tuple(jnp.concatenate([blocks_ref[c, n, part] for c in range(cores)], axis=0) for part in range(2))
+        for n in range(chunks)
+    ]
+    parts = butterfly(parts, -1.0)
+    fields = []
+    for k in range(radix):
+        cosine, sine = twiddle_ref[0, k], twiddle_ref[1, k]
+        part = parts[k] if k == 0 else turn(parts[k], cosine, -sine)
+        spectrum = table_times(back_ref, jnp.concatenate(part, axis=0))
+        rows = slice(k * short, (k + 1) * short)
+        part = turn((spectrum[:short], spectrum[short:]), prop_ref[0, rows, :], prop_ref[1, rows, :])
+        field = table_times(table_ref, jnp.concatenate(part, axis=0))
+        part = (field[:short], field[short:])
+        fields.append(part if k == 0 else turn(part, cosine, sine))
+    fields = butterfly(fields, 1.0)
+    for n in range(chunks):
+        for c in range(cores):
+            for part in range(2):
+                out_ref[c, n, part] = fields[n][part][c * half:(c + 1) * half]
+
+
+def last_kernel(more, blocks_ref, slow_ref, scalars_ref, table_ref, back_ref, twiddle_ref, field_ref, *next_ref):
+    short = twiddle_ref.shape[2]
+    per_core = radix // blocks_ref.shape[0]
+    parts = [
+        tuple(blocks_ref[k // per_core, 0, part, :, pl.ds(k % per_core * short, short)] for part in range(2))
+        for k in range(radix)
+    ]
+    parts = rows_inverse(parts, back_ref, twiddle_ref[...])
+    omega, polarity = scalars_ref[0], scalars_ref[1]
+    turned = []
+    for n in range(radix):
+        lanes = slice(n * short, (n + 1) * short)
+        slow = jnp.concatenate([slow_ref[0, q, 0, :, lanes] for q in range(slow_ref.shape[1])], axis=0)
+        sine, cosine = small_sincos(polarity * omega * ((slow - reference_slowness) * depth_interval))
+        part = turn(parts[n], cosine, sine)
+        for side in range(2):
+            field_ref[0, side, :, lanes] = part[side]
+        turned.append(part)
+    if more:
+        write_spectrum(next_ref[0], rows_forward(turned, table_ref, twiddle_ref[...]))
+
+
+def one_field_per_chip(wavefields, slowness, freq_index):
+    x_rows, y_total = wavefields.shape[3:]
+    gy, fld = lax.axis_size("gy"), lax.axis_size("fld")
+    freq_devs, shots = lax.axis_size("freq"), lax.axis_size("shot")
+    x_total = x_rows * gy
+    half, width = x_rows // fld, y_total // fld
+    short = y_total // radix
+    z, core, x = lax.axis_index("gy"), lax.axis_index("fld"), lax.axis_index("freq")
+    omega = omega_unit * lax.dynamic_index_in_dim(freq_index, z // fld, keepdims=False).astype(jnp.float32)
+    polarity = (2 * (z % fld) - 1).astype(jnp.float32)
+    scalars = jnp.stack([omega, polarity])
+
+    table, back = (jnp.asarray(t) for t in split_table(short))
+    angles = twiddle_angles(y_total)
+    lane_twiddle = jnp.asarray(np.stack([np.cos(angles), np.sin(angles)]).astype(np.float32))
+    cols = min(256, width)
+    row_twiddle = jnp.broadcast_to(lane_twiddle[..., None], (2, radix, short, cols))
+
+    share = half // (freq_devs * shots)
+    mine = (lax.axis_index("shot") * freq_devs + x) * share + core * half
+    part_slow = lax.dynamic_slice_in_dim(slowness, mine, share, axis=1)
+    slow = lax.all_gather(part_slow, ("gy", "shot", "freq"), axis=0, tiled=False)
+    slow = slow.reshape(gy, freq_devs * shots, slowness.shape[0], share, y_total)
+
+    field, prop = spread(wavefields, scalars, gy, fld, x_total, y_total)
+
+    smem = pl.BlockSpec(memory_space=pltpu.SMEM)
+    whole = pl.BlockSpec((2, 2 * short, 2 * short), lambda i: (0, 0, 0))
+    lane_tw = pl.BlockSpec((2, radix, short), lambda i: (0, 0, 0))
+    field_spec = pl.BlockSpec((1, 2, half, y_total), lambda i: (i, 0, 0, 0))
+    spec_spec = pl.BlockSpec((fld, 1, 2, half, width), lambda i: (0, i, 0, 0, 0))
+    spec_shape = jax.ShapeDtypeStruct((fld, gy, 2, half, width), jnp.float32)
+    field_shape = jax.ShapeDtypeStruct((gy, 2, half, y_total), jnp.float32)
+    col_spec = pl.BlockSpec((fld, gy, 2, half, cols), lambda i: (0, 0, 0, 0, i))
+    params = pltpu.CompilerParams(vmem_limit_bytes=40 * 2**20)
+
+    spectrum = pl.pallas_call(
+        first_kernel, name="first", grid=(gy,), out_shape=spec_shape,
+        in_specs=[field_spec, whole, lane_tw], out_specs=spec_spec, compiler_params=params,
+    )(field, table, lane_twiddle)
+
+    images = []
+    for depth_step in range(DEPTH):
+        more = depth_step + 1 < DEPTH
+        blocks = lax.all_to_all(spectrum, "fld", split_axis=0, concat_axis=0, tiled=True)
+        blocks = pl.pallas_call(
+            middle_kernel, name="middle", grid=(width // cols,), out_shape=spec_shape,
+            in_specs=[
+                col_spec, pl.BlockSpec((2, x_total, cols), lambda i: (0, 0, i)), whole, whole,
+                pl.BlockSpec((2, radix, short, cols), lambda i: (0, 0, 0, 0)),
+            ],
+            out_specs=col_spec, compiler_params=params,
+        )(blocks, prop, table, back, row_twiddle)
+        blocks = lax.all_to_all(blocks, "fld", split_axis=0, concat_axis=0, tiled=True)
+        slow_spec = pl.BlockSpec(
+            (1, freq_devs * shots, 1, share, y_total), lambda i, d=depth_step: (i, 0, d, 0, 0)
+        )
+        out = pl.pallas_call(
+            functools.partial(last_kernel, more), name="last", grid=(gy,),
+            out_shape=(field_shape, spec_shape) if more else (field_shape,),
+            in_specs=[spec_spec, slow_spec, smem, whole, whole, lane_tw],
+            out_specs=(field_spec, spec_spec) if more else (field_spec,), compiler_params=params,
+        )(blocks, slow, scalars, table, back, lane_twiddle)
+        if more:
+            spectrum = out[1]
+        images.append(image_of(out[0], z, x, gy, fld, freq_devs))
+    return jnp.stack(images)
+
+
+def image_of(field, z, x, gy, fld, freq_devs):
+    _, _, half, y_total = field.shape
+    side = z % fld
+    sides = field.reshape(gy // fld, fld, 2, half, y_total)
+    sent = lax.dynamic_index_in_dim(sides, 1 - side, axis=1, keepdims=False)
+    kept = lax.dynamic_index_in_dim(sides, side, axis=1, keepdims=False)
+    other = lax.ppermute(sent, "gy", [(i, i ^ 1) for i in range(gy)])
+    term = jnp.sum(kept * other, axis=1)
+    columns = term.reshape(gy // fld, half, freq_devs, y_total // freq_devs)
+    sent = lax.dynamic_index_in_dim(columns, 1 - x, axis=2, keepdims=False)
+    kept = lax.dynamic_index_in_dim(columns, x, axis=2, keepdims=False)
+    columns = kept + lax.ppermute(sent, "freq", [(0, 1), (1, 0)])
+    sent = lax.dynamic_index_in_dim(columns, 1 - z // fld, axis=0, keepdims=False)
+    kept = lax.dynamic_index_in_dim(columns, z // fld, axis=0, keepdims=False)
+    rows = kept + lax.ppermute(sent, "gy", [(i, i ^ 2) for i in range(gy)])
+    rows = jnp.swapaxes(rows.reshape(half, fld, -1), 0, 1)
+    rows = lax.all_to_all(rows, "fld", split_axis=0, concat_axis=0, tiled=True)
+    return rows.reshape(half * fld, -1)
+
+
+def fits(mesh, wavefields):
+    shape = dict(mesh.shape)
+    freqs = wavefields.shape[2] // (shape["shot"] * shape["freq"])
+    x_total, y_total = wavefields.shape[3:]
+    return (
+        shape["gy"] == radix == freqs * shape["fld"] and shape["fld"] == 2 and shape["freq"] == 2
+        and x_total == y_total and y_total % (radix * 128) == 0
+        and x_total // shape["gy"] // shape["fld"] % (8 * shape["freq"] * shape["shot"]) == 0
+    )
+
+
 def solution(mesh):
     placed = (P("fld", None, ("shot", "freq"), "gy", None), P(None, "gy", None), P("freq"))
-    return jax.shard_map(
-        per_device,
-        mesh=mesh,
-        in_specs=placed,
-        out_specs=P("shot", "gy", ("freq", "fld")),
-        check_vma=False,
-    )
+
+    def run(wavefields, slowness, freq_index):
+        return jax.shard_map(
+            one_field_per_chip if fits(mesh, wavefields) else per_device,
+            mesh=mesh,
+            in_specs=placed,
+            out_specs=P("shot", "gy", ("freq", "fld")),
+            check_vma=False,
+        )(wavefields, slowness, freq_index)
+
+    return run

time: 686 us -> 374 us (0.55); the launches traced: 677 us -> 374 us
  waiting for transfers between devices: 284 us -> 103 us
  Pallas kernels: 0 us -> 141 us
  matrix products: 111 us -> 0 us
  local copies, waits for them, and re-layouts: 84.5 us -> 17.7 us
  other arithmetic: 63.5 us -> 10.4 us
  blocking collectives: 96.6 us -> 61.9 us
    all_to_all x4 -> x3, waiting for transfers between devices: 259 us -> 5.88 us  [the longest x1 4.47 us: one_field_per_chip(): lax.all_to_all(blocks, 'fld', split_axis=0, concat_axis=0, tiled=True)]
    pallas_call x0 -> x6, Pallas kernels: none -> 141 us  [the longest x1 90.5 us: spread(): pl.pallas_call(functools.partial(spread_kernel, (gy, fld), x_total, y_tot...]
    dot_general x16 -> x0, matrix products: 111 us -> none  [contract(): jnp.einsum(pattern, values, matrix, precision=lax.Precision.HIGHEST, pref...]
    ppermute x0 -> x6, waiting for transfers between devices: none -> 97.6 us  [the longest x2 84 us: image_of(): other = lax.ppermute(sent, 'gy', [(i, i ^ 1) for i in range(gy)])]
    sub x12 -> x0, other arithmetic: 44 us -> none  [rotate(): real_part * cosine - imag_part * sine_part]
    all_to_all x1 -> x3, blocking collectives: 96.6 us -> 61.9 us  [the longest x2 54.8 us: one_field_per_chip(): lax.all_to_all(spectrum, 'fld', split_axis=0, concat_axis=0, tiled=True)]
    another operation x14 -> x0, local copies, waits for them, and re-layouts: 33.4 us -> none  [the longest x2 14.5 us: per_device(): blocks = wave_field.reshape(2, batches, x_rows, pencils, y_cols // pencils)]
    reduce_scatter x2 -> x0, waiting for transfers between devices: 24.1 us -> none  [per_device(): lax.psum_scatter(partial_image, ('freq', 'fld'), scatter_dimension=2, til...]
  transfers between devices with their start and end apart: 6 -> 10, of which waited for: 5 -> 6; matrix products, arithmetic and copies ran while one was open for 9% -> 5% of each run, Pallas kernels for 0% -> 29%
where the time goes in v1:
time: 374 us
  Pallas kernels  141 us (38%)
  waiting for transfers between devices  103 us (28%)
  blocking collectives  61.9 us (17%)
  starting transfers between devices  25 us (7%)
  local copies, waits for them, and re-layouts  17.7 us (5%)
  between operations  14.2 us (4%)
  other arithmetic  10.4 us (3%)
    pallas_call x1, Pallas kernels, spread(): pl.pallas_call(functools.partial(spread_kernel, (gy, fld), x_total, y_tot...  90.5 us
    ppermute x2, waiting for transfers between devices, image_of(): other = lax.ppermute(sent, 'gy', [(i, i ^ 1) for i in range(gy)])  84 us
    all_to_all x2, blocking collectives, one_field_per_chip(): lax.all_to_all(spectrum, 'fld', split_axis=0, concat_axis=0, tiled=True)  54.8 us
    pallas_call x2, Pallas kernels, one_field_per_chip(): pl.pallas_call(middle_kernel, name='middle', grid=(width // cols,), out_s...  23.7 us
    pallas_call x2, Pallas kernels, one_field_per_chip(): pl.pallas_call(functools.partial(last_kernel, more), name='last', grid=(g...  22.4 us
    unnamed x22, local copies, waits for them, and re-layouts  8.92 us
    ppermute x2, starting transfers between devices, image_of(): rows = kept + lax.ppermute(sent, 'gy', [(i, i ^ 2) for i in range(gy)])  8.04 us
  transfers between devices with their start and end apart: 10, of which 6 were waited for; matrix products, arithmetic and copies ran while one was open for 5% of the time, Pallas kernels for 29%

profile of v1, /device:TPU:0, one launch (start us, length us, event | category | flops | bytes accessed | tf_op | source)
XLA Modules:
  0.0 373.6 jit_solution(15672789083428161005)
XLA Ops:
  6.5 1.6 copy-done
  10.8 2.2 copy-done.8
  13.0 90.5 %spread.1 = (f32[4,2,128,1024]{3,2,1,0:T(8,128)S(1)}, f32[2,1024,512]{2,1,0:T(8,128)S(1)}) custom-call(f32[1,2,2,256,1024]{4,3,2,1,0:T(8,128)S(1)} %copy-done.8, f32[2]{0:T(128)S(1)} %pad_maximum_fusion.1.scalars_ref), custom_call_target="tpu_custom_call" | custom-call | flops 100000000 | bytes 300000000 | tf_op jit(solution)/shard_map/spread/pallas_call | solution.py:331
  103.5 2.0 copy-done.7
  105.4 4.4 %first.1 = f32[2,4,2,128,512]{4,3,2,1,0:T(8,128)S(1)} custom-call(f32[4,2,128,1024]{3,2,1,0:T(8,128)S(1)} %get-tuple-element.9.field_ref, bf16[2,512,512]{2,1,0:T(8,128)(2,1)S(1)} %copy-done.2, f32[2,4,256]{2,1,0:T(4,128)S(1)} %copy-done.10), custom_call_target="tpu_custom_call" | custom-call | tf_op jit(solution)/shard_map/first/pallas_call | solution.py:453
  109.8 47.7 %all_to_all.30.blocks_ref = f32[2,4,2,128,512]{4,3,2,1,0:T(8,128)S(1)} all-to-all(f32[2,4,2,128,512]{4,3,2,1,0:T(8,128)S(1)} %first.1), channel_id=1, replica_groups=mesh['shot'=2,'gy'=4,'freq'=2,'fld'=2] {'fld'}, dimensions={0} | all-to-all | bytes 8388608 | tf_op jit(solution)/shard_map/all_to_all | solution.py:461
  157.9 11.8 %middle.2 = f32[2,4,2,128,512]{4,3,2,1,0:T(8,128)S(1)} custom-call(f32[2,4,2,128,512]{4,3,2,1,0:T(8,128)S(1)} %all_to_all.30.blocks_ref, f32[2,1024,512]{2,1,0:T(8,128)} %copy-done.7, bf16[2,512,512]{2,1,0:T(8,128)(2,1)S(1)} %copy-done.2, bf16[2,512,512]{2,1,0:T(8,128)(2,1)S(1)} %copy-done.3, f32[2,4,256,256]{3,2,1,0:T(8,128)S(1)} %broadcast_in_dim.2.twiddle_ref), custom_call_target="tpu_custom_call" | custom-call | tf_op jit(solution)/shard_map/middle/pallas_call | solution.py:462
  169.7 1.9 copy-done.6
  171.7 5.6 %all-to-all-start.1 = ((f32[2,4,2,128,512]{4,3,2,1,0:T(8,128)}), f32[2,4,2,128,512]{4,3,2,1,0:T(8,128)}, u32[]{:S(2)}, u32[]{:S(2)}) async-start(f32[2,4,2,128,512]{4,3,2,1,0:T(8,128)} %copy-done.6), calls=%async_computation.1 | async-start | bytes 8388608 | tf_op jit(solution)/shard_map/all_to_all | solution.py:470
  177.3 4.5 %all-to-all-done.1.blocks_ref = f32[2,4,2,128,512]{4,3,2,1,0:T(8,128)} async-done(((f32[2,4,2,128,512]{4,3,2,1,0:T(8,128)}), f32[2,4,2,128,512]{4,3,2,1,0:T(8,128)}, u32[]{:S(2)}, u32[]{:S(2)}) %all-to-all-start.1) | async-done | bytes 4194336 | tf_op jit(solution)/shard_map/all_to_all | solution.py:470
  183.0 13.5 %last.2 = (f32[4,2,128,1024]{3,2,1,0:T(8,128)S(1)}, f32[2,4,2,128,512]{4,3,2,1,0:T(8,128)S(1)}) custom-call(f32[2,4,2,128,512]{4,3,2,1,0:T(8,128)} %all-to-all-done.1.blocks_ref, f32[4,4,2,32,1024]{4,3,2,1,0:T(8,128)} %bitcast.46, f32[2]{0:T(128)S(1)} %pad_maximum_fusion.1.scalars_ref, bf16[2,512,512]{2,1,0:T(8,128)(2,1)S(1)} %copy-done.2, ...), custom_call_target="tpu_custom_call" | custom-call | tf_op jit(solution)/shard_map/last/pallas_call | solution.py:474
  196.5 7.1 %all_to_all.31.blocks_ref = f32[2,4,2,128,512]{4,3,2,1,0:T(8,128)S(1)} all-to-all(f32[2,4,2,128,512]{4,3,2,1,0:T(8,128)S(1)} %get-tuple-element.12), channel_id=1, replica_groups=mesh['shot'=2,'gy'=4,'freq'=2,'fld'=2] {'fld'}, dimensions={0} | all-to-all | bytes 8388608 | tf_op jit(solution)/shard_map/all_to_all | solution.py:461
  203.6 11.8 %middle.3 = f32[2,4,2,128,512]{4,3,2,1,0:T(8,128)S(1)} custom-call(f32[2,4,2,128,512]{4,3,2,1,0:T(8,128)S(1)} %all_to_all.31.blocks_ref, f32[2,1024,512]{2,1,0:T(8,128)} %copy-done.7, bf16[2,512,512]{2,1,0:T(8,128)(2,1)S(1)} %copy-done.2, bf16[2,512,512]{2,1,0:T(8,128)(2,1)S(1)} %copy-done.4, f32[2,4,256,256]{3,2,1,0:T(8,128)S(1)} %broadcast_in_dim.2.twiddle_ref), custom_call_target="tpu_custom_call" | custom-call | tf_op jit(solution)/shard_map/middle/pallas_call | solution.py:462
  215.5 7.1 %all_to_all.32.blocks_ref = f32[2,4,2,128,512]{4,3,2,1,0:T(8,128)S(1)} all-to-all(f32[2,4,2,128,512]{4,3,2,1,0:T(8,128)S(1)} %middle.3), channel_id=1, replica_groups=mesh['shot'=2,'gy'=4,'freq'=2,'fld'=2] {'fld'}, dimensions={0} | all-to-all | bytes 8388608 | tf_op jit(solution)/shard_map/all_to_all | solution.py:470
  222.6 8.9 %last.3 = f32[4,2,128,1024]{3,2,1,0:T(8,128)S(1)} custom-call(f32[2,4,2,128,512]{4,3,2,1,0:T(8,128)S(1)} %all_to_all.32.blocks_ref, f32[4,4,2,32,1024]{4,3,2,1,0:T(8,128)} %bitcast.47, f32[2]{0:T(128)S(1)} %pad_maximum_fusion.1.scalars_ref, bf16[2,512,512]{2,1,0:T(8,128)(2,1)S(1)} %copy-done.2, bf16[2,512,512]{2,1,0:T(8,128)(2,1)S(1)} %copy-done.4, ...), custom_call_target="tpu_custom_call" | custom-call | tf_op jit(solution)/shard_map/last/pallas_call | solution.py:474
  231.7 1.5 collective-permute-start.3
  233.3 1.6 dynamic-slice_bitcast_fusion.1
  235.6 44.8 %collective-permute-done.3 = f32[2,2,128,1024]{3,2,1,0:T(8,128)} collective-permute-done((f32[2,2,128,1024]{3,2,1,0:T(8,128)S(1)}, f32[2,2,128,1024]{3,2,1,0:T(8,128)}, u32[]{:S(2)}, u32[]{:S(2)}) %collective-permute-start.3) | collective-permute-done | bytes 2097184 | tf_op jit(solution)/shard_map/ppermute | solution.py:492
  280.4 2.7 fusion
  285.4 39.1 %collective-permute-done = f32[2,2,128,1024]{3,2,1,0:T(8,128)} collective-permute-done((f32[2,2,128,1024]{3,2,1,0:T(8,128)}, f32[2,2,128,1024]{3,2,1,0:T(8,128)}, u32[]{:S(2)}, u32[]{:S(2)}) %collective-permute-start) | collective-permute-done | bytes 2097184 | tf_op jit(solution)/shard_map/ppermute | solution.py:492
  324.5 2.7 fusion.1
  327.3 1.3 copy.9
  328.6 1.9 dynamic-slice_bitcast_fusion.3
  331.7 1.2 bitcast_add_fusion
  333.0 3.7 collective-permute-start.5
  336.6 7.3 %collective-permute-done.1 = f32[2,128,512]{1,2,0:T(8,128)} collective-permute-done((f32[2,128,512]{1,2,0:T(8,128)}, f32[2,128,512]{1,2,0:T(8,128)}, u32[]{:S(2)}, u32[]{:S(2)}) %collective-permute-start.1) | collective-permute-done | bytes 524320 | tf_op jit(solution)/shard_map/ppermute | solution.py:497
  343.9 1.3 bitcast_add_fusion.1
  345.2 4.4 %collective-permute-start.2 = (f32[128,512]{0,1:T(8,128)S(1)}, f32[128,512]{0,1:T(8,128)S(1)}, u32[]{:S(2)}, u32[]{:S(2)}) collective-permute-start(f32[128,512]{0,1:T(8,128)S(1)} %dynamic-slice_bitcast_fusion.5), channel_id=1, source_target_pairs={{0,8},{4,12},{8,0},{12,4},{1,9},{5,13},{9,1},{13,5},{2,10},{6,14},... | collective-permute-start | bytes 786440 | tf_op jit(solution)/shard_map/ppermute | solution.py:500
  350.3 3.4 all-to-all-start.5
  353.7 6.3 %collective-permute-done.2 = f32[128,512]{0,1:T(8,128)S(1)} collective-permute-done((f32[128,512]{0,1:T(8,128)S(1)}, f32[128,512]{0,1:T(8,128)S(1)}, u32[]{:S(2)}, u32[]{:S(2)}) %collective-permute-start.2) | collective-permute-done | bytes 262176 | tf_op jit(solution)/shard_map/ppermute | solution.py:500
  360.8 3.4 all-to-all-start.2
  364.4 1.4 all-to-all-done.2
  (41 shorter events, 10.6 us)
Async XLA Ops:
  6.5 1.6 copy-start
  6.5 98.9 %copy-start.2 = (bf16[2,512,512]{2,1,0:T(8,128)(2,1)S(1)}, bf16[2,512,512]{2,1,0:T(8,128)(2,1)}, u32[]{:S(2)}) copy-start(bf16[2,512,512]{2,1,0:T(8,128)(2,1)} %constant.109.clone.table_ref) | copy-start | bytes 3145732
  6.5 175.2 %all-gather.3.cloned.1.call-start = ((), (), s32[]{:S(2)}) async-start(), calls=%async_computation.6 | async-start | bytes 4456448 | tf_op jit(solution)/shard_map/all_gather | solution.py:438
  10.8 2.2 copy-start.8
  13.0 92.5 %copy-start.10 = (f32[2,4,256]{2,1,0:T(4,128)S(1)}, f32[2,4,256]{2,1,0:T(4,128)}, u32[]{:S(2)}) copy-start(f32[2,4,256]{2,1,0:T(4,128)} %constant.111.clone.twiddle_ref) | copy-start | bytes 24580
  103.5 2.0 copy-start.7
  109.8 48.1 %copy-start.3 = (bf16[2,512,512]{2,1,0:T(8,128)(2,1)S(1)}, bf16[2,512,512]{2,1,0:T(8,128)(2,1)}, u32[]{:S(2)}) copy-start(bf16[2,512,512]{2,1,0:T(8,128)(2,1)} %constant.110.clone.back_ref) | copy-start | bytes 3145732
  169.7 1.9 copy-start.6
  171.7 10.1 %all-to-all-start.1 = ((f32[2,4,2,128,512]{4,3,2,1,0:T(8,128)}), f32[2,4,2,128,512]{4,3,2,1,0:T(8,128)}, u32[]{:S(2)}, u32[]{:S(2)}) async-start(f32[2,4,2,128,512]{4,3,2,1,0:T(8,128)} %copy-done.6), calls=%async_computation.1 | async-start | bytes 8388608 | tf_op jit(solution)/shard_map/all_to_all | solution.py:470
  181.8 1.2 copy-start.4
  196.5 36.8 %copy-start.9 = (f32[4,2,128,1024]{3,2,1,0:T(8,128)}, f32[4,2,128,1024]{3,2,1,0:T(8,128)S(1)}, u32[]{:S(2)}) copy-start(f32[4,2,128,1024]{3,2,1,0:T(8,128)S(1)} %get-tuple-element.11) | copy-start | bytes 12582916
  231.5 3.4 copy-start.5
  231.7 48.7 %collective-permute-start.3 = (f32[2,2,128,1024]{3,2,1,0:T(8,128)S(1)}, f32[2,2,128,1024]{3,2,1,0:T(8,128)}, u32[]{:S(2)}, u32[]{:S(2)}) collective-permute-start(f32[2,2,128,1024]{3,2,1,0:T(8,128)S(1)} %dynamic-slice_bitcast_fusion), channel_id=1, source_target_pairs={{0,4},{4,0},{8,12},{12,8},{1,5},{5,1},{9,13},{13,9},{2,6},{6,2},{1... | collective-permute-start | bytes 6291464 | tf_op jit(solution)/shard_map/ppermute | solution.py:492
  234.9 89.7 %collective-permute-start = (f32[2,2,128,1024]{3,2,1,0:T(8,128)}, f32[2,2,128,1024]{3,2,1,0:T(8,128)}, u32[]{:S(2)}, u32[]{:S(2)}) collective-permute-start(f32[2,2,128,1024]{3,2,1,0:T(8,128)} %dynamic-slice_bitcast_fusion.1), channel_id=1, source_target_pairs={{0,4},{4,0},{8,12},{12,8},{1,5},{5,1},{9,13},{13,9},{2,6},{6,2},{1... | collective-permute-start | bytes 6291464 | tf_op jit(solution)/shard_map/ppermute | solution.py:492
  284.3 47.3 %collective-permute-start.4 = (f32[2,128,512]{1,2,0:T(8,128)}, f32[2,128,512]{1,2,0:T(8,128)}, u32[]{:S(2)}, u32[]{:S(2)}) collective-permute-start(f32[2,128,512]{1,2,0:T(8,128)} %dynamic-slice_bitcast_fusion.2), channel_id=1, source_target_pairs={{0,2},{2,0},{1,3},{3,1},{4,6},{6,4},{5,7},{7,5},{8,10},{10,8},{9,1... | collective-permute-start | bytes 1572872 | tf_op jit(solution)/shard_map/ppermute | solution.py:497
  330.5 13.4 %collective-permute-start.1 = (f32[2,128,512]{1,2,0:T(8,128)}, f32[2,128,512]{1,2,0:T(8,128)}, u32[]{:S(2)}, u32[]{:S(2)}) collective-permute-start(f32[2,128,512]{1,2,0:T(8,128)} %dynamic-slice_bitcast_fusion.3), channel_id=1, source_target_pairs={{0,2},{2,0},{1,3},{3,1},{4,6},{6,4},{5,7},{7,5},{8,10},{10,8},{9,1... | collective-permute-start | bytes 1572872 | tf_op jit(solution)/shard_map/ppermute | solution.py:497
  331.7 35.1 %copy-start.1 = (f32[2,256,1024]{2,1,0:T(8,128)S(1)}, f32[2,256,1024]{2,1,0:T(8,128)}, u32[]{:S(2)}) copy-start(f32[2,256,1024]{2,1,0:T(8,128)} %param.7) | copy-start | bytes 6291460
  333.0 16.6 %collective-permute-start.5 = (f32[128,512]{0,1:T(8,128)S(1)}, f32[128,512]{0,1:T(8,128)S(1)}, u32[]{:S(2)}, u32[]{:S(2)}) collective-permute-start(f32[128,512]{0,1:T(8,128)S(1)} %dynamic-slice_bitcast_fusion.4), channel_id=1, source_target_pairs={{0,8},{4,12},{8,0},{12,4},{1,9},{5,13},{9,1},{13,5},{2,10},{6,14},... | collective-permute-start | bytes 786440 | tf_op jit(solution)/shard_map/ppermute | solution.py:500
  345.2 14.9 %collective-permute-start.2 = (f32[128,512]{0,1:T(8,128)S(1)}, f32[128,512]{0,1:T(8,128)S(1)}, u32[]{:S(2)}, u32[]{:S(2)}) collective-permute-start(f32[128,512]{0,1:T(8,128)S(1)} %dynamic-slice_bitcast_fusion.5), channel_id=1, source_target_pairs={{0,8},{4,12},{8,0},{12,4},{1,9},{5,13},{9,1},{13,5},{2,10},{6,14},... | collective-permute-start | bytes 786440 | tf_op jit(solution)/shard_map/ppermute | solution.py:500
  350.3 10.5 %all-to-all-start.5 = ((f32[2,128,256]{1,2,0:T(8,128)}), f32[2,128,256]{1,2,0:T(8,128)S(1)}, u32[]{:S(2)}, u32[]{:S(2)}) async-start(f32[2,128,256]{1,2,0:T(8,128)} %bitcast.22), calls=%async_computation.5 | async-start | bytes 524288 | tf_op jit(solution)/shard_map/all_to_all | solution.py:502
  360.8 5.0 %all-to-all-start.2 = ((f32[2,128,256]{1,2,0:T(8,128)}), f32[2,128,256]{1,2,0:T(8,128)S(1)}, u32[]{:S(2)}, u32[]{:S(2)}) async-start(f32[2,128,256]{1,2,0:T(8,128)} %bitcast.11), calls=%async_computation.2 | async-start | bytes 524288 | tf_op jit(solution)/shard_map/all_to_all | solution.py:502
Sparse Core Ops, SparseCore 0:
  10.1 139.8 all-gather.2

commit v2 on v1

--- a/solution.py
+++ b/solution.py
@@ -161,7 +161,7 @@
     return combined.reshape(DEPTH, x_rows, column_width)
 
 
-radix = 4
+radix = 8
 MESH = pl.DeviceIdType.MESH
 
 
@@ -196,10 +196,26 @@
 
 def table_times(table, values):
     high, low = halves(values)
-    return dot32(table[0], high) + (dot32(table[0], low) + dot32(table[1], high))
+    length = table.shape[1]
+    both = dot32(jnp.concatenate([table[0], table[1]], axis=0), high)
+    return both[:length] + (both[length:] + dot32(table[0], low))
 
 
 def butterfly(parts, sign):
+    even, odd = quarter(parts[0::2], sign), quarter(parts[1::2], sign)
+    root = math.sqrt(0.5)
+    (_, _), (r1, i1), (r2, i2), (r3, i3) = odd
+    odd = [
+        odd[0],
+        (root * (r1 - sign * i1), root * (i1 + sign * r1)),
+        (-sign * i2, sign * r2),
+        (-root * (r3 + sign * i3), root * (sign * r3 - i3)),
+    ]
+    added = [(e[0] + o[0], e[1] + o[1]) for e, o in zip(even, odd)]
+    return added + [(e[0] - o[0], e[1] - o[1]) for e, o in zip(even, odd)]
+
+
+def quarter(parts, sign):
     (r0, i0), (r1, i1), (r2, i2), (r3, i3) = parts
     ar, ai, br, bi = r0 + r2, i0 + i2, r0 - r2, i0 - i2
     cr, ci, dr, di = r1 + r3, i1 + i3, r1 - r3, i1 - i3
@@ -368,12 +384,8 @@
 
 
 def middle_kernel(blocks_ref, prop_ref, table_ref, back_ref, twiddle_ref, out_ref):
-    cores, chunks, _, half, cols = blocks_ref.shape
-    short = cores * half
-    parts = [
-        tuple(jnp.concatenate([blocks_ref[c, n, part] for c in range(cores)], axis=0) for part in range(2))
-        for n in range(chunks)
-    ]
+    cores, chunks, _, short, cols = blocks_ref.shape
+    parts = [(blocks_ref[c, n, 0], blocks_ref[c, n, 1]) for n in range(chunks) for c in range(cores)]
     parts = butterfly(parts, -1.0)
     fields = []
     for k in range(radix):
@@ -389,7 +401,7 @@
     for n in range(chunks):
         for c in range(cores):
             for part in range(2):
-                out_ref[c, n, part] = fields[n][part][c * half:(c + 1) * half]
+                out_ref[c, n, part] = fields[n * cores + c][part]
 
 
 def last_kernel(more, blocks_ref, slow_ref, scalars_ref, table_ref, back_ref, twiddle_ref, field_ref, *next_ref):
@@ -404,7 +416,7 @@
     turned = []
     for n in range(radix):
         lanes = slice(n * short, (n + 1) * short)
-        slow = jnp.concatenate([slow_ref[0, q, 0, :, lanes] for q in range(slow_ref.shape[1])], axis=0)
+        slow = jnp.concatenate([slow_ref[0, q, :, lanes] for q in range(slow_ref.shape[1])], axis=0)
         sine, cosine = small_sincos(polarity * omega * ((slow - reference_slowness) * depth_interval))
         part = turn(parts[n], cosine, sine)
         for side in range(2):
@@ -435,10 +447,14 @@
     share = half // (freq_devs * shots)
     mine = (lax.axis_index("shot") * freq_devs + x) * share + core * half
     part_slow = lax.dynamic_slice_in_dim(slowness, mine, share, axis=1)
-    slow = lax.all_gather(part_slow, ("gy", "shot", "freq"), axis=0, tiled=False)
-    slow = slow.reshape(gy, freq_devs * shots, slowness.shape[0], share, y_total)
-
     field, prop = spread(wavefields, scalars, gy, fld, x_total, y_total)
+    part_slow, field = lax.optimization_barrier((part_slow, field))
+    slows = [
+        lax.all_gather(part_slow[d], ("gy", "shot", "freq"), axis=0, tiled=False).reshape(
+            gy, freq_devs * shots, share, y_total
+        )
+        for d in range(DEPTH)
+    ]
 
     smem = pl.BlockSpec(memory_space=pltpu.SMEM)
     whole = pl.BlockSpec((2, 2 * short, 2 * short), lambda i: (0, 0, 0))
@@ -449,10 +465,11 @@
     field_shape = jax.ShapeDtypeStruct((gy, 2, half, y_total), jnp.float32)
     col_spec = pl.BlockSpec((fld, gy, 2, half, cols), lambda i: (0, 0, 0, 0, i))
     params = pltpu.CompilerParams(vmem_limit_bytes=40 * 2**20)
+    cost = pl.CostEstimate(flops=12 * 2 * 2 * short * x_total * y_total // fld, bytes_accessed=12 * x_total * y_total, transcendentals=0)
 
     spectrum = pl.pallas_call(
         first_kernel, name="first", grid=(gy,), out_shape=spec_shape,
-        in_specs=[field_spec, whole, lane_tw], out_specs=spec_spec, compiler_params=params,
+        in_specs=[field_spec, whole, lane_tw], out_specs=spec_spec, compiler_params=params, cost_estimate=cost,
     )(field, table, lane_twiddle)
 
     images = []
@@ -465,18 +482,16 @@
                 col_spec, pl.BlockSpec((2, x_total, cols), lambda i: (0, 0, i)), whole, whole,
                 pl.BlockSpec((2, radix, short, cols), lambda i: (0, 0, 0, 0)),
             ],
-            out_specs=col_spec, compiler_params=params,
+            out_specs=col_spec, compiler_params=params, cost_estimate=cost,
         )(blocks, prop, table, back, row_twiddle)
         blocks = lax.all_to_all(blocks, "fld", split_axis=0, concat_axis=0, tiled=True)
-        slow_spec = pl.BlockSpec(
-            (1, freq_devs * shots, 1, share, y_total), lambda i, d=depth_step: (i, 0, d, 0, 0)
-        )
+        slow_spec = pl.BlockSpec((1, freq_devs * shots, share, y_total), lambda i: (i, 0, 0, 0))
         out = pl.pallas_call(
             functools.partial(last_kernel, more), name="last", grid=(gy,),
             out_shape=(field_shape, spec_shape) if more else (field_shape,),
             in_specs=[spec_spec, slow_spec, smem, whole, whole, lane_tw],
-            out_specs=(field_spec, spec_spec) if more else (field_spec,), compiler_params=params,
-        )(blocks, slow, scalars, table, back, lane_twiddle)
+            out_specs=(field_spec, spec_spec) if more else (field_spec,), compiler_params=params, cost_estimate=cost,
+        )(blocks, slows[depth_step], scalars, table, back, lane_twiddle)
         if more:
             spectrum = out[1]
         images.append(image_of(out[0], z, x, gy, fld, freq_devs))
@@ -508,7 +523,7 @@
     freqs = wavefields.shape[2] // (shape["shot"] * shape["freq"])
     x_total, y_total = wavefields.shape[3:]
     return (
-        shape["gy"] == radix == freqs * shape["fld"] and shape["fld"] == 2 and shape["freq"] == 2
+        shape["gy"] == 4 == freqs * shape["fld"] and shape["fld"] == 2 and shape["freq"] == 2
         and x_total == y_total and y_total % (radix * 128) == 0
         and x_total // shape["gy"] // shape["fld"] % (8 * shape["freq"] * shape["shot"]) == 0
     )

time: 374 us -> 354 us (0.947)
  Pallas kernels: 141 us -> 113 us
  blocking collectives: 61.9 us -> 44.2 us
  waiting for transfers between devices: 103 us -> 117 us
  local copies, waits for them, and re-layouts: 17.7 us -> 28.2 us
    all_gather x1 -> x2, waiting for transfers between devices: 0.01 us -> 55.2 us  [one_field_per_chip(): lax.all_gather(part_slow[d], ('gy', 'shot', 'freq'), axis=0, tiled=False)]
    ppermute x2, waiting for transfers between devices: 84 us -> 40.5 us  [image_of(): other = lax.ppermute(sent, 'gy', [(i, i ^ 1) for i in range(gy)])]
    all_to_all x2, blocking collectives: 54.8 us -> 36.1 us  [one_field_per_chip(): lax.all_to_all(spectrum, 'fld', split_axis=0, concat_axis=0, tiled=True)]
    pallas_call x1, Pallas kernels: 90.5 us -> 74.6 us  [spread(): pl.pallas_call(functools.partial(spread_kernel, (gy, fld), x_total, y_tot...]
    unnamed x22 -> x30, local copies, waits for them, and re-layouts: 8.92 us -> 17.7 us
    pallas_call x2, Pallas kernels: 23.7 us -> 15.9 us  [one_field_per_chip(): pl.pallas_call(middle_kernel, name='middle', grid=(width // cols,), out_s...]
  transfers between devices with their start and end apart: 10 -> 11, of which waited for: 6 -> 7; matrix products, arithmetic and copies ran while one was open for 5% -> 5% of each run, Pallas kernels for 29% -> 11%
where the time goes in v2:
time: 354 us
  waiting for transfers between devices  117 us (33%)
  Pallas kernels  113 us (32%)
  blocking collectives  44.2 us (12%)
  local copies, waits for them, and re-layouts  28.2 us (8%)
  starting transfers between devices  26.4 us (7%)
  between operations  14.3 us (4%)
  other arithmetic  10.4 us (3%)
    pallas_call x1, Pallas kernels, spread(): pl.pallas_call(functools.partial(spread_kernel, (gy, fld), x_total, y_tot...  74.6 us
    all_gather x2, waiting for transfers between devices, one_field_per_chip(): lax.all_gather(part_slow[d], ('gy', 'shot', 'freq'), axis=0, tiled=False)  55.2 us
    ppermute x2, waiting for transfers between devices, image_of(): other = lax.ppermute(sent, 'gy', [(i, i ^ 1) for i in range(gy)])  40.5 us
    all_to_all x2, blocking collectives, one_field_per_chip(): lax.all_to_all(spectrum, 'fld', split_axis=0, concat_axis=0, tiled=True)  36.1 us
    pallas_call x2, Pallas kernels, one_field_per_chip(): pl.pallas_call(functools.partial(last_kernel, more), name='last', grid=(g...  20 us
    unnamed x30, local copies, waits for them, and re-layouts  17.7 us
    pallas_call x2, Pallas kernels, one_field_per_chip(): pl.pallas_call(middle_kernel, name='middle', grid=(width // cols,), out_s...  15.9 us
    all_to_all x1, blocking collectives, one_field_per_chip(): lax.all_to_all(blocks, 'fld', split_axis=0, concat_axis=0, tiled=True)  8.18 us
  transfers between devices with their start and end apart: 11, of which 7 were waited for; matrix products, arithmetic and copies ran while one was open for 5% of the time, Pallas kernels for 11%

profile of v2, /device:TPU:0, one launch (start us, length us, event | category | flops | bytes accessed | tf_op | source)
XLA Modules:
  0.0 353.6 jit_solution(16454717902501606324)
XLA Ops:
  8.7 2.2 copy-done.4
  10.9 74.6 %spread.1 = (f32[4,2,128,1024]{3,2,1,0:T(8,128)S(1)}, f32[2,1024,512]{2,1,0:T(8,128)S(1)}) custom-call(f32[1,2,2,256,1024]{4,3,2,1,0:T(8,128)S(1)} %copy-done.4, f32[2]{0:T(128)S(1)} %pad_maximum_fusion.1.scalars_ref), custom_call_target="tpu_custom_call" | custom-call | flops 100000000 | bytes 300000000 | tf_op jit(solution)/shard_map/spread/pallas_call | solution.py:347
  85.5 1.9 copy-done.3
  87.4 2.0 copy-done.11
  91.0 2.2 copy-done.12
  93.2 2.8 first.1
  96.1 29.0 %all_to_all.30.blocks_ref = f32[2,4,2,128,512]{4,3,2,1,0:T(8,128)S(1)} all-to-all(f32[2,4,2,128,512]{4,3,2,1,0:T(8,128)S(1)} %first.1), channel_id=1, replica_groups=mesh['shot'=2,'gy'=4,'freq'=2,'fld'=2] {'fld'}, dimensions={0} | all-to-all | bytes 8388608 | tf_op jit(solution)/shard_map/all_to_all | solution.py:478
  125.4 7.9 %middle.2 = f32[2,4,2,128,512]{4,3,2,1,0:T(8,128)S(1)} custom-call(f32[2,4,2,128,512]{4,3,2,1,0:T(8,128)S(1)} %all_to_all.30.blocks_ref, f32[2,1024,512]{2,1,0:T(8,128)} %copy-done.3, bf16[2,256,256]{2,1,0:T(8,128)(2,1)S(1)} %copy-done.8, bf16[2,256,256]{2,1,0:T(8,128)(2,1)S(1)} %copy-done.9, f32[2,8,128,256]{3,2,1,0:T(8,128)S(1)} %broadcast_in_dim.2.twiddle_ref), custom_call_target="tpu_custom_call" | custom-call | flops 3221225472 | bytes 12582912 | tf_op jit(solution)/shard_map/middle/pallas_call | solution.py:479
  133.3 2.0 copy-done.2
  135.3 5.6 %all-to-all-start.1 = ((f32[2,4,2,128,512]{4,3,2,1,0:T(8,128)}), f32[2,4,2,128,512]{4,3,2,1,0:T(8,128)}, u32[]{:S(2)}, u32[]{:S(2)}) async-start(f32[2,4,2,128,512]{4,3,2,1,0:T(8,128)} %copy-done.2), calls=%async_computation.1 | async-start | bytes 8388608 | tf_op jit(solution)/shard_map/all_to_all | solution.py:487
  141.0 4.5 %all-to-all-done.1.blocks_ref = f32[2,4,2,128,512]{4,3,2,1,0:T(8,128)} async-done(((f32[2,4,2,128,512]{4,3,2,1,0:T(8,128)}), f32[2,4,2,128,512]{4,3,2,1,0:T(8,128)}, u32[]{:S(2)}, u32[]{:S(2)}) %all-to-all-start.1) | async-done | bytes 4194336 | tf_op jit(solution)/shard_map/all_to_all | solution.py:487
  145.4 26.8 %all-gather.3.cloned.1.call-done = f32[16,32,1024]{2,1,0:T(8,128)} async-done(((f32[1,32,1024]{2,1,0:T(8,128)}), f32[16,32,1024]{2,1,0:T(8,128)}) %all-gather.3.cloned.1.call-update) | async-done | bytes 2097168 | tf_op jit(solution)/shard_map/all_gather | solution.py:453
  173.8 13.1 %last.2 = (f32[4,2,128,1024]{3,2,1,0:T(8,128)S(1)}, f32[2,4,2,128,512]{4,3,2,1,0:T(8,128)S(1)}) custom-call(f32[2,4,2,128,512]{4,3,2,1,0:T(8,128)} %all-to-all-done.1.blocks_ref, f32[4,4,32,1024]{3,2,1,0:T(8,128)S(1)} %bitcast.48, f32[2]{0:T(128)S(1)} %pad_maximum_fusion.1.scalars_ref, bf16[2,256,256]{2,1,0:T(8,128)(2,1)S(1)} %copy-done.8, ...), custom_call_target="tpu_custom_call" | custom-call | flops 3221225472 | bytes 12582912 | tf_op jit(solution)/shard_map/last/pallas_call | solution.py:489
  186.9 1.8 dynamic-slice_bitcast_fusion.1
  190.2 7.1 %all_to_all.31.blocks_ref = f32[2,4,2,128,512]{4,3,2,1,0:T(8,128)S(1)} all-to-all(f32[2,4,2,128,512]{4,3,2,1,0:T(8,128)S(1)} %get-tuple-element.16), channel_id=1, replica_groups=mesh['shot'=2,'gy'=4,'freq'=2,'fld'=2] {'fld'}, dimensions={0} | all-to-all | bytes 8388608 | tf_op jit(solution)/shard_map/all_to_all | solution.py:478
  197.3 7.9 %middle.3 = f32[2,4,2,128,512]{4,3,2,1,0:T(8,128)S(1)} custom-call(f32[2,4,2,128,512]{4,3,2,1,0:T(8,128)S(1)} %all_to_all.31.blocks_ref, f32[2,1024,512]{2,1,0:T(8,128)} %copy-done.3, bf16[2,256,256]{2,1,0:T(8,128)(2,1)S(1)} %copy-done.8, bf16[2,256,256]{2,1,0:T(8,128)(2,1)S(1)} %copy-done.9, f32[2,8,128,256]{3,2,1,0:T(8,128)S(1)} %broadcast_in_dim.2.twiddle_ref), custom_call_target="tpu_custom_call" | custom-call | flops 3221225472 | bytes 12582912 | tf_op jit(solution)/shard_map/middle/pallas_call | solution.py:479
  205.2 8.2 %all_to_all.32.blocks_ref = f32[2,4,2,128,512]{4,3,2,1,0:T(8,128)} all-to-all(f32[2,4,2,128,512]{4,3,2,1,0:T(8,128)S(1)} %middle.3), channel_id=1, replica_groups=mesh['shot'=2,'gy'=4,'freq'=2,'fld'=2] {'fld'}, dimensions={0} | all-to-all | bytes 8388608 | tf_op jit(solution)/shard_map/all_to_all | solution.py:487
  213.4 28.4 %all-gather.5.cloned.1.call-done = f32[16,32,1024]{2,1,0:T(8,128)} async-done(((f32[1,32,1024]{2,1,0:T(8,128)}), f32[16,32,1024]{2,1,0:T(8,128)}) %all-gather.5.cloned.1.call-update) | async-done | bytes 2097168 | tf_op jit(solution)/shard_map/all_gather | solution.py:453
  241.8 2.2 copy-done.7
  245.6 6.9 %last.3 = f32[4,2,128,1024]{3,2,1,0:T(8,128)S(1)} custom-call(f32[2,4,2,128,512]{4,3,2,1,0:T(8,128)S(1)} %copy-done.7, f32[4,4,32,1024]{3,2,1,0:T(8,128)S(1)} %bitcast.47, f32[2]{0:T(128)S(1)} %pad_maximum_fusion.1.scalars_ref, bf16[2,256,256]{2,1,0:T(8,128)(2,1)S(1)} %copy-done.8, bf16[2,256,256]{2,1,0:T(8,128)(2,1)S(1)} %copy-done.9, ...), custom_call_target="tpu_custom_call" | custom-call | flops 3221225472 | bytes 12582912 | tf_op jit(solution)/shard_map/last/pallas_call | solution.py:489
  252.5 1.9 copy-done.6
  256.0 4.3 %collective-permute-start.3 = (f32[2,2,128,1024]{3,2,1,0:T(8,128)}, f32[2,2,128,1024]{3,2,1,0:T(8,128)}, u32[]{:S(2)}, u32[]{:S(2)}) collective-permute-start(f32[2,2,128,1024]{3,2,1,0:T(8,128)} %dynamic-slice_bitcast_fusion), channel_id=1, source_target_pairs={{0,4},{4,0},{8,12},{12,8},{1,5},{5,1},{9,13},{13,9},{2,6},{6,2},{1... | collective-permute-start | bytes 6291464 | tf_op jit(solution)/shard_map/ppermute | solution.py:507
  260.3 2.7 fusion.1
  265.8 40.5 %collective-permute-done.3 = f32[2,2,128,1024]{3,2,1,0:T(8,128)} collective-permute-done((f32[2,2,128,1024]{3,2,1,0:T(8,128)}, f32[2,2,128,1024]{3,2,1,0:T(8,128)}, u32[]{:S(2)}, u32[]{:S(2)}) %collective-permute-start.3) | collective-permute-done | bytes 2097184 | tf_op jit(solution)/shard_map/ppermute | solution.py:507
  306.2 2.7 fusion
  310.3 1.9 dynamic-slice_bitcast_fusion.2
  314.9 2.7 collective-permute-start.2
  317.6 7.9 %collective-permute-done.4 = f32[2,128,512]{1,2,0:T(8,128)} collective-permute-done((f32[2,128,512]{1,2,0:T(8,128)}, f32[2,128,512]{1,2,0:T(8,128)}, u32[]{:S(2)}, u32[]{:S(2)}) %collective-permute-start.4) | collective-permute-done | bytes 524320 | tf_op jit(solution)/shard_map/ppermute | solution.py:512
  326.9 2.4 collective-permute-start.5
  330.0 3.4 all-to-all-start.2
  333.5 6.5 %collective-permute-done.5 = f32[128,512]{0,1:T(8,128)S(1)} collective-permute-done((f32[128,512]{0,1:T(8,128)S(1)}, f32[128,512]{0,1:T(8,128)S(1)}, u32[]{:S(2)}, u32[]{:S(2)}) %collective-permute-start.5) | collective-permute-done | bytes 262176 | tf_op jit(solution)/shard_map/ppermute | solution.py:515
  340.8 3.4 all-to-all-start.5
  (53 shorter events, 21.5 us)
Async XLA Ops:
  6.5 82.9 %copy-start = (f32[2,256,1024]{2,1,0:T(8,128)S(1)}, f32[2,256,1024]{2,1,0:T(8,128)}, u32[]{:S(2)}) copy-start(f32[2,256,1024]{2,1,0:T(8,128)} %param.7) | copy-start | bytes 6291460
  6.5 84.5 %copy-start.10 = (f32[2,8,128]{2,1,0:T(8,128)S(1)}, f32[2,8,128]{2,1,0:T(8,128)}, u32[]{:S(2)}) copy-start(f32[2,8,128]{2,1,0:T(8,128)} %constant.111.clone.twiddle_ref) | copy-start | bytes 24580
  6.5 165.7 %all-gather.3.cloned.1.call-start = ((), (), s32[]{:S(2)}) async-start(), calls=%async_computation.6 | async-start | bytes 2228224 | tf_op jit(solution)/shard_map/all_gather | solution.py:453
  8.7 2.2 copy-start.4
  10.9 80.1 %copy-start.8 = (bf16[2,256,256]{2,1,0:T(8,128)(2,1)S(1)}, bf16[2,256,256]{2,1,0:T(8,128)(2,1)}, u32[]{:S(2)}) copy-start(bf16[2,256,256]{2,1,0:T(8,128)(2,1)} %constant.109.clone.table_ref) | copy-start | bytes 786436
  85.5 2.0 copy-start.3
  87.4 2.0 copy-start.11
  90.2 151.5 %all-gather.5.cloned.1.call-start = ((), (), s32[]{:S(2)}) async-start(), calls=%async_computation.7 | async-start | bytes 2228224 | tf_op jit(solution)/shard_map/all_gather | solution.py:453
  91.0 2.2 copy-start.12
  96.0 29.3 %copy-start.9 = (bf16[2,256,256]{2,1,0:T(8,128)(2,1)S(1)}, bf16[2,256,256]{2,1,0:T(8,128)(2,1)}, u32[]{:S(2)}) copy-start(bf16[2,256,256]{2,1,0:T(8,128)(2,1)} %constant.110.clone.back_ref) | copy-start | bytes 786436
  133.3 2.0 copy-start.2
  135.3 10.1 %all-to-all-start.1 = ((f32[2,4,2,128,512]{4,3,2,1,0:T(8,128)}), f32[2,4,2,128,512]{4,3,2,1,0:T(8,128)}, u32[]{:S(2)}, u32[]{:S(2)}) async-start(f32[2,4,2,128,512]{4,3,2,1,0:T(8,128)} %copy-done.2), calls=%async_computation.1 | async-start | bytes 8388608 | tf_op jit(solution)/shard_map/all_to_all | solution.py:487
  172.2 1.6 copy-start.14
  186.9 3.3 copy-start.5
  188.7 71.6 %collective-permute-start = (f32[2,2,128,1024]{3,2,1,0:T(8,128)}, f32[2,2,128,1024]{3,2,1,0:T(8,128)}, u32[]{:S(2)}, u32[]{:S(2)}) collective-permute-start(f32[2,2,128,1024]{3,2,1,0:T(8,128)} %dynamic-slice_bitcast_fusion.1), channel_id=1, source_target_pairs={{0,4},{4,0},{8,12},{12,8},{1,5},{5,1},{9,13},{13,9},{2,6},{6,2},{1... | collective-permute-start | bytes 6291464 | tf_op jit(solution)/shard_map/ppermute | solution.py:507
  241.8 2.2 copy-start.7
  244.0 1.6 copy-start.13
  252.5 2.0 copy-start.6
  256.0 50.2 %collective-permute-start.3 = (f32[2,2,128,1024]{3,2,1,0:T(8,128)}, f32[2,2,128,1024]{3,2,1,0:T(8,128)}, u32[]{:S(2)}, u32[]{:S(2)}) collective-permute-start(f32[2,2,128,1024]{3,2,1,0:T(8,128)} %dynamic-slice_bitcast_fusion), channel_id=1, source_target_pairs={{0,4},{4,0},{8,12},{12,8},{1,5},{5,1},{9,13},{13,9},{2,6},{6,2},{1... | collective-permute-start | bytes 6291464 | tf_op jit(solution)/shard_map/ppermute | solution.py:507
  264.3 49.4 %collective-permute-start.1 = (f32[2,128,512]{1,2,0:T(8,128)}, f32[2,128,512]{1,2,0:T(8,128)}, u32[]{:S(2)}, u32[]{:S(2)}) collective-permute-start(f32[2,128,512]{1,2,0:T(8,128)} %dynamic-slice_bitcast_fusion.3), channel_id=1, source_target_pairs={{0,2},{2,0},{1,3},{3,1},{4,6},{6,4},{5,7},{7,5},{8,10},{10,8},{9,1... | collective-permute-start | bytes 1572872 | tf_op jit(solution)/shard_map/ppermute | solution.py:512
  312.2 13.4 %collective-permute-start.4 = (f32[2,128,512]{1,2,0:T(8,128)}, f32[2,128,512]{1,2,0:T(8,128)}, u32[]{:S(2)}, u32[]{:S(2)}) collective-permute-start(f32[2,128,512]{1,2,0:T(8,128)} %dynamic-slice_bitcast_fusion.2), channel_id=1, source_target_pairs={{0,2},{2,0},{1,3},{3,1},{4,6},{6,4},{5,7},{7,5},{8,10},{10,8},{9,1... | collective-permute-start | bytes 1572872 | tf_op jit(solution)/shard_map/ppermute | solution.py:512
  313.7 33.1 %copy-start.1 = (f32[2,256,1024]{2,1,0:T(8,128)S(1)}, f32[2,256,1024]{2,1,0:T(8,128)}, u32[]{:S(2)}) copy-start(f32[2,256,1024]{2,1,0:T(8,128)} %param.7) | copy-start | bytes 6291460
  314.9 14.3 %collective-permute-start.2 = (f32[128,512]{0,1:T(8,128)S(1)}, f32[128,512]{0,1:T(8,128)S(1)}, u32[]{:S(2)}, u32[]{:S(2)}) collective-permute-start(f32[128,512]{0,1:T(8,128)S(1)} %dynamic-slice_bitcast_fusion.5), channel_id=1, source_target_pairs={{0,8},{4,12},{8,0},{12,4},{1,9},{5,13},{9,1},{13,5},{2,10},{6,14},... | collective-permute-start | bytes 786440 | tf_op jit(solution)/shard_map/ppermute | solution.py:515
  326.9 13.2 %collective-permute-start.5 = (f32[128,512]{0,1:T(8,128)S(1)}, f32[128,512]{0,1:T(8,128)S(1)}, u32[]{:S(2)}, u32[]{:S(2)}) collective-permute-start(f32[128,512]{0,1:T(8,128)S(1)} %dynamic-slice_bitcast_fusion.4), channel_id=1, source_target_pairs={{0,8},{4,12},{8,0},{12,4},{1,9},{5,13},{9,1},{13,5},{2,10},{6,14},... | collective-permute-start | bytes 786440 | tf_op jit(solution)/shard_map/ppermute | solution.py:515
  330.0 10.7 %all-to-all-start.2 = ((f32[2,128,256]{1,2,0:T(8,128)}), f32[2,128,256]{1,2,0:T(8,128)S(1)}, u32[]{:S(2)}, u32[]{:S(2)}) async-start(f32[2,128,256]{1,2,0:T(8,128)} %bitcast.11), calls=%async_computation.2 | async-start | bytes 524288 | tf_op jit(solution)/shard_map/all_to_all | solution.py:517
  340.8 5.0 %all-to-all-start.5 = ((f32[2,128,256]{1,2,0:T(8,128)}), f32[2,128,256]{1,2,0:T(8,128)S(1)}, u32[]{:S(2)}, u32[]{:S(2)}) async-start(f32[2,128,256]{1,2,0:T(8,128)} %bitcast.23), calls=%async_computation.5 | async-start | bytes 524288 | tf_op jit(solution)/shard_map/all_to_all | solution.py:517
Sparse Core Ops, SparseCore 0:
  90.4 81.8 all-gather.2
  175.0 66.7 all-gather.4

commit v3 on v2

--- a/solution.py
+++ b/solution.py
@@ -256,8 +256,12 @@
     return angle * sine, cosine
 
 
-def spread_kernel(axes, x_total, y_total, step_rows, fields_ref, scalars_ref, out_ref, prop_ref, send_sem, recv_sem, self_sem):
-    gy, fld = axes
+def spread_kernel(axes, x_total, y_total, step_rows, fields_ref, slow_ref, scalars_ref, out_ref, slow_out, prop_ref,
+                  send_sem, recv_sem, self_sem, near_send, near_recv, far_send, far_recv, slow_sem):
+    gy, fld, freq_devs, shots = axes
+    x, shot = lax.axis_index("freq"), lax.axis_index("shot")
+    share = slow_out.shape[3]
+    my_share = shot * freq_devs + x
     me, core = lax.axis_index("gy"), lax.axis_index("fld")
     freqs = fields_ref.shape[2]
     half = out_ref.shape[2]
@@ -269,7 +273,55 @@
                     barrier, inc=1, device_id_type=MESH,
                     device_id={"gy": lax.rem(me + dz, gy), "fld": lax.rem(core + dc, fld)},
                 )
-    pl.semaphore_wait(barrier, gy * fld - 1)
+    others = [(ds, dx) for ds in range(shots) for dx in range(freq_devs) if ds + dx > 0]
+
+    def peer(ds, dx):
+        return {"shot": lax.rem(shot + ds, shots), "freq": lax.rem(x + dx, freq_devs)}
+
+    for ds, dx in others:
+        pl.semaphore_signal(barrier, inc=1, device_id_type=MESH, device_id=peer(ds, dx))
+    pl.semaphore_wait(barrier, gy * fld - 1 + len(others))
+
+    def near(dz):
+        rows = pl.ds(pl.multiple_of(core * half + my_share * share, share), share)
+        return pltpu.make_async_remote_copy(
+            src_ref=slow_ref.at[:, rows, :], dst_ref=slow_out.at[me, my_share],
+            send_sem=near_send.at[dz - 1], recv_sem=near_recv.at[dz - 1],
+            device_id={"gy": lax.rem(me + dz, gy)}, device_id_type=MESH,
+        )
+
+    def far(dz, n):
+        piece = slow_out.at[lax.rem(me - dz + gy, gy), my_share]
+        return pltpu.make_async_remote_copy(
+            src_ref=piece, dst_ref=piece, send_sem=far_send.at[dz - 1, n], recv_sem=far_recv.at[dz - 1, n],
+            device_id=peer(*others[n]), device_id_type=MESH,
+        )
+
+    def near_wait(dz):
+        piece = slow_out.at[lax.rem(me - dz + gy, gy), my_share]
+        pltpu.make_async_remote_copy(
+            src_ref=piece, dst_ref=piece, send_sem=near_send.at[dz - 1], recv_sem=near_recv.at[dz - 1],
+            device_id={"gy": lax.rem(me + dz, gy)}, device_id_type=MESH,
+        ).wait_recv()
+
+    def far_wait(dz, n):
+        ds, dx = others[n]
+        share_of = lax.rem(shot - ds + shots, shots) * freq_devs + lax.rem(x - dx + freq_devs, freq_devs)
+        piece = slow_out.at[lax.rem(me - dz + gy, gy), share_of]
+        pltpu.make_async_remote_copy(
+            src_ref=piece, dst_ref=piece, send_sem=far_send.at[dz - 1, n], recv_sem=far_recv.at[dz - 1, n],
+            device_id=peer(ds, dx), device_id_type=MESH,
+        ).wait_recv()
+
+    local = [
+        pltpu.make_async_copy(
+            slow_ref.at[:, pl.ds(pl.multiple_of(core * half + q * share, share), share), :],
+            slow_out.at[me, q], slow_sem.at[q],
+        )
+        for q in range(freq_devs * shots)
+    ]
+    for dz in range(1, gy):
+        near(dz).start()
 
     def remote(f, h):
         return pltpu.make_async_remote_copy(
@@ -297,6 +349,9 @@
     @pl.when(is_mine)
     def _():
         own.start()
+
+    for copy in local:
+        copy.start()
 
     omega, polarity = scalars_ref[0], scalars_ref[1]
     x_short, y_short = x_total // radix, y_total // radix
@@ -318,6 +373,11 @@
         prop_ref[0, pl.ds(start, step_rows), :] = amplitude * (1.0 - 2.0 * sine * sine)
         prop_ref[1, pl.ds(start, step_rows), :] = amplitude * (2.0 * sine * cosine)
 
+    for dz in range(1, gy):
+        near_wait(dz)
+        for n in range(len(others)):
+            far(dz, n).start()
+
     for f, h in order:
         mine = jnp.logical_and(f * fld + core == me, core == h)
 
@@ -340,27 +400,46 @@
     def _():
         own.wait()
 
-
-def spread(fields, scalars, gy, fld, x_total, y_total):
+    for copy in local:
+        copy.wait()
+    for dz in range(1, gy):
+        near(dz).wait_send()
+        for n in range(len(others)):
+            far_wait(dz, n)
+            far(dz, n).wait_send()
+
+
+def spread(fields, slowness, scalars, axes, x_total, y_total):
+    gy, fld, freq_devs, shots = axes
     half = fields.shape[3] // fld
     width = y_total // fld
     return pl.pallas_call(
-        functools.partial(spread_kernel, (gy, fld), x_total, y_total, 16),
+        functools.partial(spread_kernel, axes, x_total, y_total, 16),
         name="spread",
         out_shape=(
             jax.ShapeDtypeStruct((gy, 2, half, y_total), jnp.float32),
+            jax.ShapeDtypeStruct(
+                (gy, freq_devs * shots, slowness.shape[0], half // (freq_devs * shots), y_total), jnp.float32
+            ),
             jax.ShapeDtypeStruct((2, x_total, width), jnp.float32),
         ),
-        in_specs=[pl.BlockSpec(memory_space=pl.ANY), pl.BlockSpec(memory_space=pltpu.SMEM)],
-        out_specs=(pl.BlockSpec(memory_space=pl.ANY), pl.BlockSpec(memory_space=pltpu.VMEM)),
+        in_specs=[pl.BlockSpec(memory_space=pl.ANY), pl.BlockSpec(memory_space=pl.ANY), pl.BlockSpec(memory_space=pltpu.SMEM)],
+        out_specs=(
+            pl.BlockSpec(memory_space=pl.ANY), pl.BlockSpec(memory_space=pl.ANY), pl.BlockSpec(memory_space=pltpu.VMEM)
+        ),
         scratch_shapes=[
             pltpu.SemaphoreType.DMA((fields.shape[2] * fld,)),
             pltpu.SemaphoreType.DMA((gy,)),
             pltpu.SemaphoreType.DMA,
+            pltpu.SemaphoreType.DMA((gy - 1,)),
+            pltpu.SemaphoreType.DMA((gy - 1,)),
+            pltpu.SemaphoreType.DMA((gy - 1, freq_devs * shots - 1)),
+            pltpu.SemaphoreType.DMA((gy - 1, freq_devs * shots - 1)),
+            pltpu.SemaphoreType.DMA((freq_devs * shots,)),
         ],
         compiler_params=pltpu.CompilerParams(collective_id=0, has_side_effects=True, vmem_limit_bytes=16 * 2**20),
         cost_estimate=pl.CostEstimate(flops=10**8, bytes_accessed=3 * 10**8, transcendentals=10**6),
-    )(fields, scalars)
+    )(fields, slowness, scalars)
 
 
 def write_spectrum(out_ref, spectra):
@@ -416,7 +495,7 @@
     turned = []
     for n in range(radix):
         lanes = slice(n * short, (n + 1) * short)
-        slow = jnp.concatenate([slow_ref[0, q, :, lanes] for q in range(slow_ref.shape[1])], axis=0)
+        slow = jnp.concatenate([slow_ref[0, q, 0, :, lanes] for q in range(slow_ref.shape[1])], axis=0)
         sine, cosine = small_sincos(polarity * omega * ((slow - reference_slowness) * depth_interval))
         part = turn(parts[n], cosine, sine)
         for side in range(2):
@@ -445,16 +524,7 @@
     row_twiddle = jnp.broadcast_to(lane_twiddle[..., None], (2, radix, short, cols))
 
     share = half // (freq_devs * shots)
-    mine = (lax.axis_index("shot") * freq_devs + x) * share + core * half
-    part_slow = lax.dynamic_slice_in_dim(slowness, mine, share, axis=1)
-    field, prop = spread(wavefields, scalars, gy, fld, x_total, y_total)
-    part_slow, field = lax.optimization_barrier((part_slow, field))
-    slows = [
-        lax.all_gather(part_slow[d], ("gy", "shot", "freq"), axis=0, tiled=False).reshape(
-            gy, freq_devs * shots, share, y_total
-        )
-        for d in range(DEPTH)
-    ]
+    field, slow, prop = spread(wavefields, slowness, scalars, (gy, fld, freq_devs, shots), x_total, y_total)
 
     smem = pl.BlockSpec(memory_space=pltpu.SMEM)
     whole = pl.BlockSpec((2, 2 * short, 2 * short), lambda i: (0, 0, 0))
@@ -485,13 +555,15 @@
             out_specs=col_spec, compiler_params=params, cost_estimate=cost,
         )(blocks, prop, table, back, row_twiddle)
         blocks = lax.all_to_all(blocks, "fld", split_axis=0, concat_axis=0, tiled=True)
-        slow_spec = pl.BlockSpec((1, freq_devs * shots, share, y_total), lambda i: (i, 0, 0, 0))
+        slow_spec = pl.BlockSpec(
+            (1, freq_devs * shots, 1, share, y_total), lambda i, d=depth_step: (i, 0, d, 0, 0)
+        )
         out = pl.pallas_call(
             functools.partial(last_kernel, more), name="last", grid=(gy,),
             out_shape=(field_shape, spec_shape) if more else (field_shape,),
             in_specs=[spec_spec, slow_spec, smem, whole, whole, lane_tw],
             out_specs=(field_spec, spec_spec) if more else (field_spec,), compiler_params=params, cost_estimate=cost,
-        )(blocks, slows[depth_step], scalars, table, back, lane_twiddle)
+        )(blocks, slow, scalars, table, back, lane_twiddle)
         if more:
             spectrum = out[1]
         images.append(image_of(out[0], z, x, gy, fld, freq_devs))

time: 354 us -> 338 us (0.955)
  Pallas kernels: 113 us -> 138 us
  between operations: 14.3 us -> 0.82 us
  waiting for transfers between devices: 117 us -> 106 us
  starting transfers between devices: 26.4 us -> 17.8 us
  local copies, waits for them, and re-layouts: 28.2 us -> 22.3 us
    all_gather x2 -> x0, waiting for transfers between devices: 55.2 us -> none  [one_field_per_chip(): lax.all_gather(part_slow[d], ('gy', 'shot', 'freq'), axis=0, tiled=False)]
    ppermute x2, waiting for transfers between devices: 40.5 us -> 82.7 us  [image_of(): other = lax.ppermute(sent, 'gy', [(i, i ^ 1) for i in range(gy)])]
    pallas_call x1, Pallas kernels: 74.6 us -> 99 us  [spread(): pl.pallas_call(functools.partial(spread_kernel, axes, x_total, y_total, 1...]
    ppermute x2, starting transfers between devices: 5.76 us -> 0.07 us  [image_of(): other = lax.ppermute(sent, 'gy', [(i, i ^ 1) for i in range(gy)])]
    unnamed x30 -> x24, local copies, waits for them, and re-layouts: 17.7 us -> 17.3 us
  transfers between devices with their start and end apart: 11 -> 9, of which waited for: 7 -> 7; matrix products, arithmetic and copies ran while one was open for 5% -> 3% of each run, Pallas kernels for 11% -> 0%
where the time goes in v3:
time: 338 us; the launch traced here: 337 us
  Pallas kernels  138 us (41%)
  waiting for transfers between devices  106 us (31%)
  blocking collectives  42.2 us (12%)
  local copies, waits for them, and re-layouts  22.3 us (7%)
  starting transfers between devices  17.8 us (5%)
  other arithmetic  9.01 us (3%)
    pallas_call x1, Pallas kernels, spread(): pl.pallas_call(functools.partial(spread_kernel, axes, x_total, y_total, 1...  99 us
    ppermute x2, waiting for transfers between devices, image_of(): other = lax.ppermute(sent, 'gy', [(i, i ^ 1) for i in range(gy)])  82.7 us
    all_to_all x2, blocking collectives, one_field_per_chip(): lax.all_to_all(spectrum, 'fld', split_axis=0, concat_axis=0, tiled=True)  35.1 us
    pallas_call x2, Pallas kernels, one_field_per_chip(): pl.pallas_call(functools.partial(last_kernel, more), name='last', grid=(g...  20.6 us
    unnamed x24, local copies, waits for them, and re-layouts  17.3 us
    pallas_call x2, Pallas kernels, one_field_per_chip(): pl.pallas_call(middle_kernel, name='middle', grid=(width // cols,), out_s...  15.9 us
    ppermute x2, waiting for transfers between devices, image_of(): columns = kept + lax.ppermute(sent, 'freq', [(0, 1), (1, 0)])  9.41 us
    ppermute x2, waiting for transfers between devices, image_of(): rows = kept + lax.ppermute(sent, 'gy', [(i, i ^ 2) for i in range(gy)])  8.65 us
  transfers between devices with their start and end apart: 9, of which 7 were waited for; matrix products, arithmetic and copies ran while one was open for 3% of the time, Pallas kernels for 0%

profile of v3, /device:TPU:0, one launch (start us, length us, event | category | flops | bytes accessed | tf_op | source)
XLA Modules:
  0.0 336.8 jit_solution(17987360986366725104)
XLA Ops:
  0.0 1.2 dynamic_slice.43
  1.9 2.2 copy-done.3
  4.1 1.6 copy-done.10
  5.7 99.0 %spread.1 = (f32[4,2,128,1024]{3,2,1,0:T(8,128)S(1)}, f32[4,4,2,32,1024]{4,3,2,1,0:T(8,128)S(1)}, f32[2,1024,512]{2,1,0:T(8,128)S(1)}) custom-call(f32[1,2,2,256,1024]{4,3,2,1,0:T(8,128)S(1)} %copy-done.3, f32[2,256,1024]{2,1,0:T(8,128)S(1)} %copy-done.10, f32[2]{0:T(128)S(1)} %pad_maximum_fusion.1.scalars_ref), custom_call_target="tpu_custom_call" | custom-call | flops 100000000 | bytes 300000000 | tf_op jit(solution)/shard_map/spread/pallas_call | solution.py:416
  104.7 2.0 copy-done.2
  106.6 2.0 copy-done.6
  108.6 2.8 first.1
  111.5 28.0 %all_to_all.30.blocks_ref = f32[2,4,2,128,512]{4,3,2,1,0:T(8,128)S(1)} all-to-all(f32[2,4,2,128,512]{4,3,2,1,0:T(8,128)S(1)} %first.1), channel_id=1, replica_groups=mesh['shot'=2,'gy'=4,'freq'=2,'fld'=2] {'fld'}, dimensions={0} | all-to-all | bytes 8388608 | tf_op jit(solution)/shard_map/all_to_all | solution.py:548
  139.8 7.9 %middle.2 = f32[2,4,2,128,512]{4,3,2,1,0:T(8,128)S(1)} custom-call(f32[2,4,2,128,512]{4,3,2,1,0:T(8,128)S(1)} %all_to_all.30.blocks_ref, f32[2,1024,512]{2,1,0:T(8,128)} %copy-done.2, bf16[2,256,256]{2,1,0:T(8,128)(2,1)S(1)} %copy-done.8, bf16[2,256,256]{2,1,0:T(8,128)(2,1)S(1)} %copy-done.9, f32[2,8,128,256]{3,2,1,0:T(8,128)S(1)} %broadcast_in_dim.2.twiddle_ref), custom_call_target="tpu_custom_call" | custom-call | flops 3221225472 | bytes 12582912 | tf_op jit(solution)/shard_map/middle/pallas_call | solution.py:549
  147.7 7.1 %all_to_all.31.blocks_ref = f32[2,4,2,128,512]{4,3,2,1,0:T(8,128)S(1)} all-to-all(f32[2,4,2,128,512]{4,3,2,1,0:T(8,128)S(1)} %middle.2), channel_id=1, replica_groups=mesh['shot'=2,'gy'=4,'freq'=2,'fld'=2] {'fld'}, dimensions={0} | all-to-all | bytes 8388608 | tf_op jit(solution)/shard_map/all_to_all | solution.py:557
  154.8 13.1 %last.2 = (f32[4,2,128,1024]{3,2,1,0:T(8,128)S(1)}, f32[2,4,2,128,512]{4,3,2,1,0:T(8,128)S(1)}) custom-call(f32[2,4,2,128,512]{4,3,2,1,0:T(8,128)S(1)} %all_to_all.31.blocks_ref, f32[4,4,2,32,1024]{4,3,2,1,0:T(8,128)} %copy-done.6, f32[2]{0:T(128)S(1)} %pad_maximum_fusion.1.scalars_ref, bf16[2,256,256]{2,1,0:T(8,128)(2,1)S(1)} %copy-done.8, ...), custom_call_target="tpu_custom_call" | custom-call | flops 3221225472 | bytes 12582912 | tf_op jit(solution)/shard_map/last/pallas_call | solution.py:561
  168.0 1.9 copy-done.4
  169.9 7.1 %all_to_all.32.blocks_ref = f32[2,4,2,128,512]{4,3,2,1,0:T(8,128)S(1)} all-to-all(f32[2,4,2,128,512]{4,3,2,1,0:T(8,128)S(1)} %get-tuple-element.14), channel_id=1, replica_groups=mesh['shot'=2,'gy'=4,'freq'=2,'fld'=2] {'fld'}, dimensions={0} | all-to-all | bytes 8388608 | tf_op jit(solution)/shard_map/all_to_all | solution.py:548
  177.0 7.9 %middle.3 = f32[2,4,2,128,512]{4,3,2,1,0:T(8,128)S(1)} custom-call(f32[2,4,2,128,512]{4,3,2,1,0:T(8,128)S(1)} %all_to_all.32.blocks_ref, f32[2,1024,512]{2,1,0:T(8,128)} %copy-done.2, bf16[2,256,256]{2,1,0:T(8,128)(2,1)S(1)} %copy-done.8, bf16[2,256,256]{2,1,0:T(8,128)(2,1)S(1)} %copy-done.9, f32[2,8,128,256]{3,2,1,0:T(8,128)S(1)} %broadcast_in_dim.2.twiddle_ref), custom_call_target="tpu_custom_call" | custom-call | flops 3221225472 | bytes 12582912 | tf_op jit(solution)/shard_map/middle/pallas_call | solution.py:549
  184.9 1.9 copy-done.1
  186.8 5.8 %all-to-all-start.4 = ((f32[2,4,2,128,512]{4,3,2,1,0:T(8,128)}), f32[2,4,2,128,512]{4,3,2,1,0:T(8,128)}, u32[]{:S(2)}, u32[]{:S(2)}) async-start(f32[2,4,2,128,512]{4,3,2,1,0:T(8,128)} %copy-done.1), calls=%async_computation.4 | async-start | bytes 8388608 | tf_op jit(solution)/shard_map/all_to_all | solution.py:557
  192.7 4.3 %all-to-all-done.4.blocks_ref = f32[2,4,2,128,512]{4,3,2,1,0:T(8,128)} async-done(((f32[2,4,2,128,512]{4,3,2,1,0:T(8,128)}), f32[2,4,2,128,512]{4,3,2,1,0:T(8,128)}, u32[]{:S(2)}, u32[]{:S(2)}) %all-to-all-start.4) | async-done | bytes 4194336 | tf_op jit(solution)/shard_map/all_to_all | solution.py:557
  197.0 2.2 copy-done.7
  199.2 7.5 %last.3 = f32[4,2,128,1024]{3,2,1,0:T(8,128)S(1)} custom-call(f32[2,4,2,128,512]{4,3,2,1,0:T(8,128)} %all-to-all-done.4.blocks_ref, f32[4,4,2,32,1024]{4,3,2,1,0:T(8,128)S(1)} %copy-done.7, f32[2]{0:T(128)S(1)} %pad_maximum_fusion.1.scalars_ref, bf16[2,256,256]{2,1,0:T(8,128)(2,1)S(1)} %copy-done.8, bf16[2,256,256]{2,1,0:T(8,128)(2,1)S(1)} %copy-done.9, ...), custom_call_target="tpu_custom_call" | custom-call | flops 3221225472 | bytes 12582912 | tf_op jit(solution)/shard_map/last/pallas_call | solution.py:561
  206.9 3.5 %copy-done.5 = f32[4,2,128,1024]{3,2,1,0:T(8,128)S(1)} copy-done((f32[4,2,128,1024]{3,2,1,0:T(8,128)S(1)}, f32[4,2,128,1024]{3,2,1,0:T(8,128)}, u32[]{:S(2)}) %copy-start.5) | copy-done | bytes 4194328
  210.4 1.5 dynamic-slice_bitcast_fusion.1
  211.9 43.6 %collective-permute-done.3 = f32[2,2,128,1024]{3,2,1,0:T(8,128)} collective-permute-done((f32[2,2,128,1024]{3,2,1,0:T(8,128)S(1)}, f32[2,2,128,1024]{3,2,1,0:T(8,128)}, u32[]{:S(2)}, u32[]{:S(2)}) %collective-permute-start.3) | collective-permute-done | bytes 2097184 | tf_op jit(solution)/shard_map/ppermute | solution.py:579
  255.5 2.7 fusion
  260.6 39.1 %collective-permute-done = f32[2,2,128,1024]{3,2,1,0:T(8,128)} collective-permute-done((f32[2,2,128,1024]{3,2,1,0:T(8,128)}, f32[2,2,128,1024]{3,2,1,0:T(8,128)}, u32[]{:S(2)}, u32[]{:S(2)}) %collective-permute-start) | collective-permute-done | bytes 2097184 | tf_op jit(solution)/shard_map/ppermute | solution.py:579
  299.7 2.7 fusion.1
  305.2 1.5 collective-permute-start.5
  306.6 9.4 %collective-permute-done.1 = f32[2,128,512]{1,2,0:T(8,128)S(1)} collective-permute-done((f32[2,128,512]{1,2,0:T(8,128)S(1)}, f32[2,128,512]{1,2,0:T(8,128)S(1)}, u32[]{:S(2)}, u32[]{:S(2)}) %collective-permute-start.1) | collective-permute-done | bytes 524320 | tf_op jit(solution)/shard_map/ppermute | solution.py:584
  317.3 7.3 %collective-permute-done.5 = f32[128,512]{0,1:T(8,128)S(1)} collective-permute-done((f32[128,512]{0,1:T(8,128)S(1)}, f32[128,512]{0,1:T(8,128)S(1)}, u32[]{:S(2)}, u32[]{:S(2)}) %collective-permute-start.5) | collective-permute-done | bytes 262176 | tf_op jit(solution)/shard_map/ppermute | solution.py:587
  325.3 3.4 %all-to-all-start.5 = ((f32[2,128,256]{1,2,0:T(8,128)}), f32[2,128,256]{1,2,0:T(8,128)S(1)}, u32[]{:S(2)}, u32[]{:S(2)}) async-start(f32[2,128,256]{1,2,0:T(8,128)} %bitcast.21), calls=%async_computation.5 | async-start | bytes 524288 | tf_op jit(solution)/shard_map/all_to_all | solution.py:589
  328.8 1.3 collective-permute-done.2
  330.8 3.4 %all-to-all-start.2 = ((f32[2,128,256]{1,2,0:T(8,128)}), f32[2,128,256]{1,2,0:T(8,128)S(1)}, u32[]{:S(2)}, u32[]{:S(2)}) async-start(f32[2,128,256]{1,2,0:T(8,128)} %bitcast.10), calls=%async_computation.2 | async-start | bytes 524288 | tf_op jit(solution)/shard_map/all_to_all | solution.py:589
  334.4 1.4 all-to-all-done.2
  (39 shorter events, 9.4 us)
Async XLA Ops:
  0.0 108.6 %copy-start.11 = (f32[2,8,128]{2,1,0:T(8,128)S(1)}, f32[2,8,128]{2,1,0:T(8,128)}, u32[]{:S(2)}) copy-start(f32[2,8,128]{2,1,0:T(8,128)} %constant.98.clone.twiddle_ref) | copy-start | bytes 24580
  1.9 2.2 copy-start.3
  4.1 1.6 copy-start.10
  5.7 102.9 %copy-start.8 = (bf16[2,256,256]{2,1,0:T(8,128)(2,1)S(1)}, bf16[2,256,256]{2,1,0:T(8,128)(2,1)}, u32[]{:S(2)}) copy-start(bf16[2,256,256]{2,1,0:T(8,128)(2,1)} %constant.96.clone.table_ref) | copy-start | bytes 786436
  104.7 2.0 copy-start.2
  106.6 2.0 copy-start.6
  111.5 28.3 %copy-start.9 = (bf16[2,256,256]{2,1,0:T(8,128)(2,1)S(1)}, bf16[2,256,256]{2,1,0:T(8,128)(2,1)}, u32[]{:S(2)}) copy-start(bf16[2,256,256]{2,1,0:T(8,128)(2,1)} %constant.97.clone.back_ref) | copy-start | bytes 786436
  167.9 1.9 copy-start.4
  184.9 1.9 copy-start.1
  186.8 10.1 %all-to-all-start.4 = ((f32[2,4,2,128,512]{4,3,2,1,0:T(8,128)}), f32[2,4,2,128,512]{4,3,2,1,0:T(8,128)}, u32[]{:S(2)}, u32[]{:S(2)}) async-start(f32[2,4,2,128,512]{4,3,2,1,0:T(8,128)} %copy-done.1), calls=%async_computation.4 | async-start | bytes 8388608 | tf_op jit(solution)/shard_map/all_to_all | solution.py:557
  197.0 2.2 copy-start.7
  206.7 5.2 %copy-start = (f32[4,2,128,1024]{3,2,1,0:T(8,128)}, f32[4,2,128,1024]{3,2,1,0:T(8,128)S(1)}, u32[]{:S(2)}) copy-start(f32[4,2,128,1024]{3,2,1,0:T(8,128)S(1)} %last.3) | copy-start | bytes 12582916
  206.7 3.7 %copy-start.5 = (f32[4,2,128,1024]{3,2,1,0:T(8,128)S(1)}, f32[4,2,128,1024]{3,2,1,0:T(8,128)}, u32[]{:S(2)}) copy-start(f32[4,2,128,1024]{3,2,1,0:T(8,128)} %copy-done.4) | copy-start | bytes 12582916
  206.9 48.7 %collective-permute-start.3 = (f32[2,2,128,1024]{3,2,1,0:T(8,128)S(1)}, f32[2,2,128,1024]{3,2,1,0:T(8,128)}, u32[]{:S(2)}, u32[]{:S(2)}) collective-permute-start(f32[2,2,128,1024]{3,2,1,0:T(8,128)S(1)} %dynamic-slice_bitcast_fusion), channel_id=1, source_target_pairs={{0,4},{4,0},{8,12},{12,8},{1,5},{5,1},{9,13},{13,9},{2,6},{6,2},{1... | collective-permute-start | bytes 6291464 | tf_op jit(solution)/shard_map/ppermute | solution.py:579
  211.9 87.8 %collective-permute-start = (f32[2,2,128,1024]{3,2,1,0:T(8,128)}, f32[2,2,128,1024]{3,2,1,0:T(8,128)}, u32[]{:S(2)}, u32[]{:S(2)}) collective-permute-start(f32[2,2,128,1024]{3,2,1,0:T(8,128)} %dynamic-slice_bitcast_fusion.1), channel_id=1, source_target_pairs={{0,4},{4,0},{8,12},{12,8},{1,5},{5,1},{9,13},{13,9},{2,6},{6,2},{1... | collective-permute-start | bytes 6291464 | tf_op jit(solution)/shard_map/ppermute | solution.py:579
  259.4 44.6 %collective-permute-start.4 = (f32[2,128,512]{1,2,0:T(8,128)}, f32[2,128,512]{1,2,0:T(8,128)}, u32[]{:S(2)}, u32[]{:S(2)}) collective-permute-start(f32[2,128,512]{1,2,0:T(8,128)} %dynamic-slice_bitcast_fusion.2), channel_id=1, source_target_pairs={{0,2},{2,0},{1,3},{3,1},{4,6},{6,4},{5,7},{7,5},{8,10},{10,8},{9,1... | collective-permute-start | bytes 1572872 | tf_op jit(solution)/shard_map/ppermute | solution.py:584
  302.8 13.2 %collective-permute-start.1 = (f32[2,128,512]{1,2,0:T(8,128)S(1)}, f32[2,128,512]{1,2,0:T(8,128)S(1)}, u32[]{:S(2)}, u32[]{:S(2)}) collective-permute-start(f32[2,128,512]{1,2,0:T(8,128)S(1)} %dynamic-slice_bitcast_fusion.3), channel_id=1, source_target_pairs={{0,2},{2,0},{1,3},{3,1},{4,6},{6,4},{5,7},{7,5},{8,10},{10,8},{9,1... | collective-permute-start | bytes 1572872 | tf_op jit(solution)/shard_map/ppermute | solution.py:584
  305.2 19.4 %collective-permute-start.5 = (f32[128,512]{0,1:T(8,128)S(1)}, f32[128,512]{0,1:T(8,128)S(1)}, u32[]{:S(2)}, u32[]{:S(2)}) collective-permute-start(f32[128,512]{0,1:T(8,128)S(1)} %dynamic-slice_bitcast_fusion.4), channel_id=1, source_target_pairs={{0,8},{4,12},{8,0},{12,4},{1,9},{5,13},{9,1},{13,5},{2,10},{6,14},... | collective-permute-start | bytes 786440 | tf_op jit(solution)/shard_map/ppermute | solution.py:587
  316.1 14.0 %collective-permute-start.2 = (f32[128,512]{0,1:T(8,128)S(1)}, f32[128,512]{0,1:T(8,128)S(1)}, u32[]{:S(2)}, u32[]{:S(2)}) collective-permute-start(f32[128,512]{0,1:T(8,128)S(1)} %dynamic-slice_bitcast_fusion.5), channel_id=1, source_target_pairs={{0,8},{4,12},{8,0},{12,4},{1,9},{5,13},{9,1},{13,5},{2,10},{6,14},... | collective-permute-start | bytes 786440 | tf_op jit(solution)/shard_map/ppermute | solution.py:587
  325.3 5.5 %all-to-all-start.5 = ((f32[2,128,256]{1,2,0:T(8,128)}), f32[2,128,256]{1,2,0:T(8,128)S(1)}, u32[]{:S(2)}, u32[]{:S(2)}) async-start(f32[2,128,256]{1,2,0:T(8,128)} %bitcast.21), calls=%async_computation.5 | async-start | bytes 524288 | tf_op jit(solution)/shard_map/all_to_all | solution.py:589
  330.8 5.0 %all-to-all-start.2 = ((f32[2,128,256]{1,2,0:T(8,128)}), f32[2,128,256]{1,2,0:T(8,128)S(1)}, u32[]{:S(2)}, u32[]{:S(2)}) async-start(f32[2,128,256]{1,2,0:T(8,128)} %bitcast.10), calls=%async_computation.2 | async-start | bytes 524288 | tf_op jit(solution)/shard_map/all_to_all | solution.py:589

commit v4 on v3

--- a/solution.py
+++ b/solution.py
@@ -463,7 +463,7 @@
 
 
 def middle_kernel(blocks_ref, prop_ref, table_ref, back_ref, twiddle_ref, out_ref):
-    cores, chunks, _, short, cols = blocks_ref.shape
+    cores, chunks, _, short, _ = blocks_ref.shape
     parts = [(blocks_ref[c, n, 0], blocks_ref[c, n, 1]) for n in range(chunks) for c in range(cores)]
     parts = butterfly(parts, -1.0)
     fields = []
@@ -512,7 +512,7 @@
     x_total = x_rows * gy
     half, width = x_rows // fld, y_total // fld
     short = y_total // radix
-    z, core, x = lax.axis_index("gy"), lax.axis_index("fld"), lax.axis_index("freq")
+    z, x = lax.axis_index("gy"), lax.axis_index("freq")
     omega = omega_unit * lax.dynamic_index_in_dim(freq_index, z // fld, keepdims=False).astype(jnp.float32)
     polarity = (2 * (z % fld) - 1).astype(jnp.float32)
     scalars = jnp.stack([omega, polarity])
@@ -546,14 +546,15 @@
     for depth_step in range(DEPTH):
         more = depth_step + 1 < DEPTH
         blocks = lax.all_to_all(spectrum, "fld", split_axis=0, concat_axis=0, tiled=True)
-        blocks = pl.pallas_call(
+        middle = pl.pallas_call(
             middle_kernel, name="middle", grid=(width // cols,), out_shape=spec_shape,
             in_specs=[
                 col_spec, pl.BlockSpec((2, x_total, cols), lambda i: (0, 0, i)), whole, whole,
                 pl.BlockSpec((2, radix, short, cols), lambda i: (0, 0, 0, 0)),
             ],
             out_specs=col_spec, compiler_params=params, cost_estimate=cost,
-        )(blocks, prop, table, back, row_twiddle)
+        )
+        blocks = middle(blocks, prop, table, back, row_twiddle)
         blocks = lax.all_to_all(blocks, "fld", split_axis=0, concat_axis=0, tiled=True)
         slow_spec = pl.BlockSpec(
             (1, freq_devs * shots, 1, share, y_total), lambda i, d=depth_step: (i, 0, d, 0, 0)
@@ -577,17 +578,20 @@
     sent = lax.dynamic_index_in_dim(sides, 1 - side, axis=1, keepdims=False)
     kept = lax.dynamic_index_in_dim(sides, side, axis=1, keepdims=False)
     other = lax.ppermute(sent, "gy", [(i, i ^ 1) for i in range(gy)])
+    width = y_total // freq_devs
     term = jnp.sum(kept * other, axis=1)
-    columns = term.reshape(gy // fld, half, freq_devs, y_total // freq_devs)
-    sent = lax.dynamic_index_in_dim(columns, 1 - x, axis=2, keepdims=False)
-    kept = lax.dynamic_index_in_dim(columns, x, axis=2, keepdims=False)
+    sent = lax.dynamic_slice_in_dim(term, (1 - x) * width, width, axis=2)
+    kept = lax.dynamic_slice_in_dim(term, x * width, width, axis=2)
     columns = kept + lax.ppermute(sent, "freq", [(0, 1), (1, 0)])
     sent = lax.dynamic_index_in_dim(columns, 1 - z // fld, axis=0, keepdims=False)
     kept = lax.dynamic_index_in_dim(columns, z // fld, axis=0, keepdims=False)
     rows = kept + lax.ppermute(sent, "gy", [(i, i ^ 2) for i in range(gy)])
-    rows = jnp.swapaxes(rows.reshape(half, fld, -1), 0, 1)
-    rows = lax.all_to_all(rows, "fld", split_axis=0, concat_axis=0, tiled=True)
-    return rows.reshape(half * fld, -1)
+    core, width = lax.axis_index("fld"), width // fld
+    sent = lax.dynamic_slice_in_dim(rows, (1 - core) * width, width, axis=1)
+    kept = lax.dynamic_slice_in_dim(rows, core * width, width, axis=1)
+    other = lax.ppermute(sent, "fld", [(0, 1), (1, 0)])
+    first = core == 0
+    return jnp.concatenate([jnp.where(first, kept, other), jnp.where(first, other, kept)], axis=0)
 
 
 def fits(mesh, wavefields):
@@ -605,12 +609,14 @@
     placed = (P("fld", None, ("shot", "freq"), "gy", None), P(None, "gy", None), P("freq"))
 
     def run(wavefields, slowness, freq_index):
-        return jax.shard_map(
-            one_field_per_chip if fits(mesh, wavefields) else per_device,
+        engaged = fits(mesh, wavefields)
+        step = jax.shard_map(
+            one_field_per_chip if engaged else per_device,
             mesh=mesh,
             in_specs=placed,
             out_specs=P("shot", "gy", ("freq", "fld")),
             check_vma=False,
-        )(wavefields, slowness, freq_index)
+        )
+        return step(wavefields, slowness, freq_index)
 
     return run

time: 338 us -> 334 us (0.988)
  waiting for transfers between devices: 106 us -> 113 us
  starting transfers between devices: 17.8 us -> 11 us
    all_to_all x2 -> x0, starting transfers between devices: 6.89 us -> none  [image_of(): rows = lax.all_to_all(rows, 'fld', split_axis=0, concat_axis=0, tiled=True)]
    ppermute x2, waiting for transfers between devices: 8.65 us -> 12.7 us  [image_of(): rows = kept + lax.ppermute(sent, 'gy', [(i, i ^ 2) for i in range(gy)])]
    unnamed x24 -> x26, local copies, waits for them, and re-layouts: 17.3 us -> 16.6 us
  transfers between devices with their start and end apart: 9 -> 9, of which waited for: 7 -> 7; matrix products, arithmetic and copies ran while one was open for 3% -> 2% of each run, Pallas kernels for 0% -> 0%
where the time goes in v4:
time: 334 us; the launch traced here: 333 us
  Pallas kernels  138 us (41%)
  waiting for transfers between devices  113 us (34%)
  blocking collectives  42.2 us (13%)
  local copies, waits for them, and re-layouts  21 us (6%)
  starting transfers between devices  11 us (3%)
  other arithmetic  7.15 us (2%)
    pallas_call x1, Pallas kernels, spread(): pl.pallas_call(functools.partial(spread_kernel, axes, x_total, y_total, 1...  99 us
    ppermute x2, waiting for transfers between devices, image_of(): other = lax.ppermute(sent, 'gy', [(i, i ^ 1) for i in range(gy)])  85.1 us
    all_to_all x2, blocking collectives, one_field_per_chip(): lax.all_to_all(spectrum, 'fld', split_axis=0, concat_axis=0, tiled=True)  35.1 us
    pallas_call x2, Pallas kernels, one_field_per_chip(): pl.pallas_call(functools.partial(last_kernel, more), name='last', grid=(g...  20.6 us
    unnamed x26, local copies, waits for them, and re-layouts  16.6 us
    pallas_call x2, Pallas kernels, one_field_per_chip(): blocks = middle(blocks, prop, table, back, row_twiddle)  15.9 us
    ppermute x2, waiting for transfers between devices, image_of(): rows = kept + lax.ppermute(sent, 'gy', [(i, i ^ 2) for i in range(gy)])  12.7 us
    ppermute x2, waiting for transfers between devices, image_of(): columns = kept + lax.ppermute(sent, 'freq', [(0, 1), (1, 0)])  9.39 us
  transfers between devices with their start and end apart: 9, of which 7 were waited for; matrix products, arithmetic and copies ran while one was open for 2% of the time, Pallas kernels for 0%

profile of v4, /device:TPU:0, one launch (start us, length us, event | category | flops | bytes accessed | tf_op | source)
XLA Modules:
  0.0 333.2 jit_solution(2865073913351997323)
XLA Ops:
  0.0 1.3 dynamic_slice.54
  2.0 2.2 copy-done.3
  4.2 1.6 copy-done.11
  5.8 99.0 %spread.1 = (f32[4,2,128,1024]{3,2,1,0:T(8,128)S(1)}, f32[4,4,2,32,1024]{4,3,2,1,0:T(8,128)S(1)}, f32[2,1024,512]{2,1,0:T(8,128)S(1)}) custom-call(f32[1,2,2,256,1024]{4,3,2,1,0:T(8,128)S(1)} %copy-done.3, f32[2,256,1024]{2,1,0:T(8,128)S(1)} %copy-done.11, f32[2]{0:T(128)S(1)} %pad_maximum_fusion.1.scalars_ref), custom_call_target="tpu_custom_call" | custom-call | flops 100000000 | bytes 300000000 | tf_op jit(solution)/shard_map/spread/pallas_call | solution.py:416
  104.7 2.0 copy-done.2
  106.7 2.0 copy-done.7
  108.7 2.8 first.1
  111.6 28.0 %all_to_all.20.blocks_ref = f32[2,4,2,128,512]{4,3,2,1,0:T(8,128)S(1)} all-to-all(f32[2,4,2,128,512]{4,3,2,1,0:T(8,128)S(1)} %first.1), channel_id=1, replica_groups=mesh['shot'=2,'gy'=4,'freq'=2,'fld'=2] {'fld'}, dimensions={0} | all-to-all | bytes 8388608 | tf_op jit(solution)/shard_map/all_to_all | solution.py:548
  139.9 7.9 %middle.2 = f32[2,4,2,128,512]{4,3,2,1,0:T(8,128)S(1)} custom-call(f32[2,4,2,128,512]{4,3,2,1,0:T(8,128)S(1)} %all_to_all.20.blocks_ref, f32[2,1024,512]{2,1,0:T(8,128)} %copy-done.2, bf16[2,256,256]{2,1,0:T(8,128)(2,1)S(1)} %copy-done.9, bf16[2,256,256]{2,1,0:T(8,128)(2,1)S(1)} %copy-done.10, f32[2,8,128,256]{3,2,1,0:T(8,128)S(1)} %broadcast_in_dim.2.twiddle_ref), custom_call_target="tpu_custom_call" | custom-call | flops 3221225472 | bytes 12582912 | tf_op jit(solution)/shard_map/middle/pallas_call | solution.py:557
  147.8 7.1 %all_to_all.21.blocks_ref = f32[2,4,2,128,512]{4,3,2,1,0:T(8,128)S(1)} all-to-all(f32[2,4,2,128,512]{4,3,2,1,0:T(8,128)S(1)} %middle.2), channel_id=1, replica_groups=mesh['shot'=2,'gy'=4,'freq'=2,'fld'=2] {'fld'}, dimensions={0} | all-to-all | bytes 8388608 | tf_op jit(solution)/shard_map/all_to_all | solution.py:558
  154.9 13.1 %last.2 = (f32[4,2,128,1024]{3,2,1,0:T(8,128)S(1)}, f32[2,4,2,128,512]{4,3,2,1,0:T(8,128)S(1)}) custom-call(f32[2,4,2,128,512]{4,3,2,1,0:T(8,128)S(1)} %all_to_all.21.blocks_ref, f32[4,4,2,32,1024]{4,3,2,1,0:T(8,128)} %copy-done.7, f32[2]{0:T(128)S(1)} %pad_maximum_fusion.1.scalars_ref, bf16[2,256,256]{2,1,0:T(8,128)(2,1)S(1)} %copy-done.9, ...), custom_call_target="tpu_custom_call" | custom-call | flops 3221225472 | bytes 12582912 | tf_op jit(solution)/shard_map/last/pallas_call | solution.py:562
  168.0 1.9 copy-done.4
  170.0 7.1 %all_to_all.22.blocks_ref = f32[2,4,2,128,512]{4,3,2,1,0:T(8,128)S(1)} all-to-all(f32[2,4,2,128,512]{4,3,2,1,0:T(8,128)S(1)} %get-tuple-element.14), channel_id=1, replica_groups=mesh['shot'=2,'gy'=4,'freq'=2,'fld'=2] {'fld'}, dimensions={0} | all-to-all | bytes 8388608 | tf_op jit(solution)/shard_map/all_to_all | solution.py:548
  177.1 7.9 %middle.3 = f32[2,4,2,128,512]{4,3,2,1,0:T(8,128)S(1)} custom-call(f32[2,4,2,128,512]{4,3,2,1,0:T(8,128)S(1)} %all_to_all.22.blocks_ref, f32[2,1024,512]{2,1,0:T(8,128)} %copy-done.2, bf16[2,256,256]{2,1,0:T(8,128)(2,1)S(1)} %copy-done.9, bf16[2,256,256]{2,1,0:T(8,128)(2,1)S(1)} %copy-done.10, f32[2,8,128,256]{3,2,1,0:T(8,128)S(1)} %broadcast_in_dim.2.twiddle_ref), custom_call_target="tpu_custom_call" | custom-call | flops 3221225472 | bytes 12582912 | tf_op jit(solution)/shard_map/middle/pallas_call | solution.py:557
  185.0 1.9 copy-done.1
  186.9 5.8 %all-to-all-start.3 = ((f32[2,4,2,128,512]{4,3,2,1,0:T(8,128)}), f32[2,4,2,128,512]{4,3,2,1,0:T(8,128)}, u32[]{:S(2)}, u32[]{:S(2)}) async-start(f32[2,4,2,128,512]{4,3,2,1,0:T(8,128)} %copy-done.1), calls=%async_computation.3 | async-start | bytes 8388608 | tf_op jit(solution)/shard_map/all_to_all | solution.py:558
  192.8 4.3 %all-to-all-done.3.blocks_ref = f32[2,4,2,128,512]{4,3,2,1,0:T(8,128)} async-done(((f32[2,4,2,128,512]{4,3,2,1,0:T(8,128)}), f32[2,4,2,128,512]{4,3,2,1,0:T(8,128)}, u32[]{:S(2)}, u32[]{:S(2)}) %all-to-all-start.3) | async-done | bytes 4194336 | tf_op jit(solution)/shard_map/all_to_all | solution.py:558
  197.1 2.2 copy-done.8
  199.3 7.5 %last.3 = f32[4,2,128,1024]{3,2,1,0:T(8,128)S(1)} custom-call(f32[2,4,2,128,512]{4,3,2,1,0:T(8,128)} %all-to-all-done.3.blocks_ref, f32[4,4,2,32,1024]{4,3,2,1,0:T(8,128)S(1)} %copy-done.8, f32[2]{0:T(128)S(1)} %pad_maximum_fusion.1.scalars_ref, bf16[2,256,256]{2,1,0:T(8,128)(2,1)S(1)} %copy-done.9, bf16[2,256,256]{2,1,0:T(8,128)(2,1)S(1)} %copy-done.10, ...), custom_call_target="tpu_custom_call" | custom-call | flops 3221225472 | bytes 12582912 | tf_op jit(solution)/shard_map/last/pallas_call | solution.py:562
  206.8 1.6 dynamic-slice_bitcast_fusion
  208.4 2.8 copy-done.5
  211.6 45.7 %collective-permute-done.4 = f32[2,2,128,1024]{3,2,1,0:T(8,128)} collective-permute-done((f32[2,2,128,1024]{3,2,1,0:T(8,128)}, f32[2,2,128,1024]{3,2,1,0:T(8,128)}, u32[]{:S(2)}, u32[]{:S(2)}) %collective-permute-start.4) | collective-permute-done | bytes 2097184 | tf_op jit(solution)/shard_map/ppermute | solution.py:580
  257.2 2.7 fusion
  260.8 1.2 collective-permute-start.5
  262.0 39.4 %collective-permute-done = f32[2,2,128,1024]{3,2,1,0:T(8,128)} collective-permute-done((f32[2,2,128,1024]{3,2,1,0:T(8,128)S(1)}, f32[2,2,128,1024]{3,2,1,0:T(8,128)}, u32[]{:S(2)}, u32[]{:S(2)}) %collective-permute-start) | collective-permute-done | bytes 2097184 | tf_op jit(solution)/shard_map/ppermute | solution.py:580
  301.4 2.1 fusion.1
  303.6 1.2 collective-permute-start.1
  306.0 1.5 collective-permute-start.6
  307.4 9.4 %collective-permute-done.1 = f32[2,128,512]{2,1,0:T(8,128)S(1)} collective-permute-done((f32[2,128,512]{2,1,0:T(8,128)S(1)}, f32[2,128,512]{2,1,0:T(8,128)S(1)}, u32[]{:S(2)}, u32[]{:S(2)}) %collective-permute-start.1) | collective-permute-done | bytes 524320 | tf_op jit(solution)/shard_map/ppermute | solution.py:585
  318.0 7.3 %collective-permute-done.6 = f32[128,512]{1,0:T(8,128)S(1)} collective-permute-done((f32[128,512]{1,0:T(8,128)S(1)}, f32[128,512]{1,0:T(8,128)S(1)}, u32[]{:S(2)}, u32[]{:S(2)}) %collective-permute-start.6) | collective-permute-done | bytes 262176 | tf_op jit(solution)/shard_map/ppermute | solution.py:588
  325.5 5.4 %collective-permute-done.2 = f32[128,512]{1,0:T(8,128)S(1)} collective-permute-done((f32[128,512]{1,0:T(8,128)S(1)}, f32[128,512]{1,0:T(8,128)S(1)}, u32[]{:S(2)}, u32[]{:S(2)}) %collective-permute-start.2) | collective-permute-done | bytes 262176 | tf_op jit(solution)/shard_map/ppermute | solution.py:588
  331.1 1.3 collective-permute-done.3
  (43 shorter events, 5.2 us)
Async XLA Ops:
  0.0 108.7 %copy-start.12 = (f32[2,8,128]{2,1,0:T(8,128)S(1)}, f32[2,8,128]{2,1,0:T(8,128)}, u32[]{:S(2)}) copy-start(f32[2,8,128]{2,1,0:T(8,128)} %constant.96.clone.twiddle_ref) | copy-start | bytes 24580
  2.0 2.2 copy-start.3
  4.2 1.6 copy-start.11
  5.8 102.9 %copy-start.9 = (bf16[2,256,256]{2,1,0:T(8,128)(2,1)S(1)}, bf16[2,256,256]{2,1,0:T(8,128)(2,1)}, u32[]{:S(2)}) copy-start(bf16[2,256,256]{2,1,0:T(8,128)(2,1)} %constant.94.clone.table_ref) | copy-start | bytes 786436
  104.7 2.0 copy-start.2
  106.7 2.0 copy-start.7
  111.5 28.3 %copy-start.10 = (bf16[2,256,256]{2,1,0:T(8,128)(2,1)S(1)}, bf16[2,256,256]{2,1,0:T(8,128)(2,1)}, u32[]{:S(2)}) copy-start(bf16[2,256,256]{2,1,0:T(8,128)(2,1)} %constant.95.clone.back_ref) | copy-start | bytes 786436
  168.0 1.9 copy-start.4
  185.0 1.9 copy-start.1
  186.9 10.1 %all-to-all-start.3 = ((f32[2,4,2,128,512]{4,3,2,1,0:T(8,128)}), f32[2,4,2,128,512]{4,3,2,1,0:T(8,128)}, u32[]{:S(2)}, u32[]{:S(2)}) async-start(f32[2,4,2,128,512]{4,3,2,1,0:T(8,128)} %copy-done.1), calls=%async_computation.3 | async-start | bytes 8388608 | tf_op jit(solution)/shard_map/all_to_all | solution.py:558
  197.1 2.2 copy-start.8
  206.8 4.7 %copy-start = (f32[4,2,128,1024]{3,2,1,0:T(8,128)}, f32[4,2,128,1024]{3,2,1,0:T(8,128)S(1)}, u32[]{:S(2)}) copy-start(f32[4,2,128,1024]{3,2,1,0:T(8,128)S(1)} %last.3) | copy-start | bytes 12582916
  206.8 4.4 %copy-start.5 = (f32[4,2,128,1024]{3,2,1,0:T(8,128)S(1)}, f32[4,2,128,1024]{3,2,1,0:T(8,128)}, u32[]{:S(2)}) copy-start(f32[4,2,128,1024]{3,2,1,0:T(8,128)} %copy-done.4) | copy-start | bytes 12582916
  208.4 48.8 %collective-permute-start.4 = (f32[2,2,128,1024]{3,2,1,0:T(8,128)}, f32[2,2,128,1024]{3,2,1,0:T(8,128)}, u32[]{:S(2)}, u32[]{:S(2)}) collective-permute-start(f32[2,2,128,1024]{3,2,1,0:T(8,128)} %dynamic-slice_bitcast_fusion), channel_id=1, source_target_pairs={{0,4},{4,0},{8,12},{12,8},{1,5},{5,1},{9,13},{13,9},{2,6},{6,2},{1... | collective-permute-start | bytes 6291464 | tf_op jit(solution)/shard_map/ppermute | solution.py:580
  211.5 89.9 %collective-permute-start = (f32[2,2,128,1024]{3,2,1,0:T(8,128)S(1)}, f32[2,2,128,1024]{3,2,1,0:T(8,128)}, u32[]{:S(2)}, u32[]{:S(2)}) collective-permute-start(f32[2,2,128,1024]{3,2,1,0:T(8,128)S(1)} %dynamic-slice_bitcast_fusion.1), channel_id=1, source_target_pairs={{0,4},{4,0},{8,12},{12,8},{1,5},{5,1},{9,13},{13,9},{2,6},{6,2},{1... | collective-permute-start | bytes 6291464 | tf_op jit(solution)/shard_map/ppermute | solution.py:580
  211.5 89.8 %copy-start.6 = (f32[4,2,128,1024]{3,2,1,0:T(8,128)S(1)}, f32[4,2,128,1024]{3,2,1,0:T(8,128)}, u32[]{:S(2)}) copy-start(f32[4,2,128,1024]{3,2,1,0:T(8,128)} %copy-done.4) | copy-start | bytes 12582916
  260.8 44.0 %collective-permute-start.5 = (f32[2,128,512]{2,1,0:T(8,128)}, f32[2,128,512]{2,1,0:T(8,128)}, u32[]{:S(2)}, u32[]{:S(2)}) collective-permute-start(f32[2,128,512]{2,1,0:T(8,128)} %constant_dynamic-slice_fusion.1), channel_id=1, source_target_pairs={{0,2},{2,0},{1,3},{3,1},{4,6},{6,4},{5,7},{7,5},{8,10},{10,8},{9,1... | collective-permute-start | bytes 1572872 | tf_op jit(solution)/shard_map/ppermute | solution.py:585
  303.6 13.2 %collective-permute-start.1 = (f32[2,128,512]{2,1,0:T(8,128)S(1)}, f32[2,128,512]{2,1,0:T(8,128)S(1)}, u32[]{:S(2)}, u32[]{:S(2)}) collective-permute-start(f32[2,128,512]{2,1,0:T(8,128)S(1)} %constant_dynamic-slice_fusion.3), channel_id=1, source_target_pairs={{0,2},{2,0},{1,3},{3,1},{4,6},{6,4},{5,7},{7,5},{8,10},{10,8},{9,1... | collective-permute-start | bytes 1572872 | tf_op jit(solution)/shard_map/ppermute | solution.py:585
  306.0 19.4 %collective-permute-start.6 = (f32[128,512]{1,0:T(8,128)S(1)}, f32[128,512]{1,0:T(8,128)S(1)}, u32[]{:S(2)}, u32[]{:S(2)}) collective-permute-start(f32[128,512]{1,0:T(8,128)S(1)} %dynamic-slice_bitcast_fusion.2), channel_id=1, source_target_pairs={{0,8},{4,12},{8,0},{12,4},{1,9},{5,13},{9,1},{13,5},{2,10},{6,14},... | collective-permute-start | bytes 786440 | tf_op jit(solution)/shard_map/ppermute | solution.py:588
  316.9 14.0 %collective-permute-start.2 = (f32[128,512]{1,0:T(8,128)S(1)}, f32[128,512]{1,0:T(8,128)S(1)}, u32[]{:S(2)}, u32[]{:S(2)}) collective-permute-start(f32[128,512]{1,0:T(8,128)S(1)} %dynamic-slice_bitcast_fusion.3), channel_id=1, source_target_pairs={{0,8},{4,12},{8,0},{12,4},{1,9},{5,13},{9,1},{13,5},{2,10},{6,14},... | collective-permute-start | bytes 786440 | tf_op jit(solution)/shard_map/ppermute | solution.py:588
  325.4 5.6 %collective-permute-start.7 = (f32[128,256]{1,0:T(8,128)S(1)}, f32[128,256]{1,0:T(8,128)S(1)}, u32[]{:S(2)}, u32[]{:S(2)}) collective-permute-start(f32[128,256]{1,0:T(8,128)S(1)} %constant_dynamic-slice_fusion), channel_id=1, source_target_pairs={{0,1},{1,0},{2,3},{3,2},{4,5},{5,4},{6,7},{7,6},{8,9},{9,8},{10,11... | collective-permute-start | bytes 393224 | tf_op jit(solution)/shard_map/ppermute | solution.py:592
  330.9 1.4 collective-permute-start.3

commit v5 on v4

--- a/solution.py
+++ b/solution.py
@@ -572,21 +572,29 @@
 
 
 def image_of(field, z, x, gy, fld, freq_devs):
-    _, _, half, y_total = field.shape
-    side = z % fld
-    sides = field.reshape(gy // fld, fld, 2, half, y_total)
-    sent = lax.dynamic_index_in_dim(sides, 1 - side, axis=1, keepdims=False)
-    kept = lax.dynamic_index_in_dim(sides, side, axis=1, keepdims=False)
-    other = lax.ppermute(sent, "gy", [(i, i ^ 1) for i in range(gy)])
+    _, _, _, y_total = field.shape
+    side, group = z % fld, z // fld
+    core = lax.axis_index("fld")
     width = y_total // freq_devs
-    term = jnp.sum(kept * other, axis=1)
-    sent = lax.dynamic_slice_in_dim(term, (1 - x) * width, width, axis=2)
-    kept = lax.dynamic_slice_in_dim(term, x * width, width, axis=2)
-    columns = kept + lax.ppermute(sent, "freq", [(0, 1), (1, 0)])
-    sent = lax.dynamic_index_in_dim(columns, 1 - z // fld, axis=0, keepdims=False)
-    kept = lax.dynamic_index_in_dim(columns, z // fld, axis=0, keepdims=False)
-    rows = kept + lax.ppermute(sent, "gy", [(i, i ^ 2) for i in range(gy)])
-    core, width = lax.axis_index("fld"), width // fld
+
+    def block(i, side):
+        return lax.dynamic_index_in_dim(field, i * fld + side, axis=0, keepdims=False)
+
+    def swapped(i, after=None):
+        sent = block(i, 1 - side)
+        other = lax.ppermute(sent, "gy", [(i, i ^ 1) for i in range(gy)])
+        if after is not None:
+            other, _ = lax.optimization_barrier((other, after))
+        term = jnp.sum(block(i, side) * other, axis=0)
+        sent = lax.dynamic_slice_in_dim(term, (1 - x) * width, width, axis=1)
+        kept = lax.dynamic_slice_in_dim(term, x * width, width, axis=1)
+        return kept + lax.ppermute(sent, "freq", [(0, 1), (1, 0)])
+
+    leaving = swapped(1 - group)
+    arrived = lax.ppermute(leaving, "gy", [(i, i ^ 2) for i in range(gy)])
+    staying = swapped(group, leaving)
+    rows = staying + arrived
+    width = width // fld
     sent = lax.dynamic_slice_in_dim(rows, (1 - core) * width, width, axis=1)
     kept = lax.dynamic_slice_in_dim(rows, core * width, width, axis=1)
     other = lax.ppermute(sent, "fld", [(0, 1), (1, 0)])

time: 334 us -> 301 us (0.901)
  waiting for transfers between devices: 113 us -> 79.1 us
  local copies, waits for them, and re-layouts: 21 us -> 16.1 us
  starting transfers between devices: 11 us -> 15.8 us
    ppermute x6 -> x10, waiting for transfers between devices: 107 us -> 73.4 us  [the longest x4 67.2 us: swapped(): other = lax.ppermute(sent, 'gy', [(i, i ^ 1) for i in range(gy)])]
    ppermute x6 -> x10, starting transfers between devices: 5.02 us -> 10.1 us  [the longest x4 4.87 us: swapped(): return kept + lax.ppermute(sent, 'freq', [(0, 1), (1, 0)])]
    unnamed x26 -> x22, local copies, waits for them, and re-layouts: 16.6 us -> 12.4 us
    reduce_sum x2 -> x4, other arithmetic: 4.88 us -> 6.7 us  [swapped(): term = jnp.sum(block(i, side) * other, axis=0)]
  transfers between devices with their start and end apart: 9 -> 13, of which waited for: 7 -> 6; matrix products, arithmetic and copies ran while one was open for 2% -> 2% of each run, Pallas kernels for 0% -> 5%
where the time goes in v5:
time: 301 us; the launch traced here: 300 us
  Pallas kernels  138 us (46%)
  waiting for transfers between devices  79.1 us (26%)
  blocking collectives  42.4 us (14%)
  local copies, waits for them, and re-layouts  16.1 us (5%)
  starting transfers between devices  15.8 us (5%)
  other arithmetic  7.89 us (3%)
    pallas_call x1, Pallas kernels, spread(): pl.pallas_call(functools.partial(spread_kernel, axes, x_total, y_total, 1...  99 us
    ppermute x4, waiting for transfers between devices, swapped(): other = lax.ppermute(sent, 'gy', [(i, i ^ 1) for i in range(gy)])  67.2 us
    all_to_all x2, blocking collectives, one_field_per_chip(): lax.all_to_all(spectrum, 'fld', split_axis=0, concat_axis=0, tiled=True)  35.1 us
    pallas_call x2, Pallas kernels, one_field_per_chip(): pl.pallas_call(functools.partial(last_kernel, more), name='last', grid=(g...  20.3 us
    pallas_call x2, Pallas kernels, one_field_per_chip(): blocks = middle(blocks, prop, table, back, row_twiddle)  15.9 us
    unnamed x22, local copies, waits for them, and re-layouts  12.4 us
    all_to_all x1, blocking collectives, one_field_per_chip(): lax.all_to_all(blocks, 'fld', split_axis=0, concat_axis=0, tiled=True)  7.37 us
    reduce_sum x4, other arithmetic, swapped(): term = jnp.sum(block(i, side) * other, axis=0)  6.7 us
  transfers between devices with their start and end apart: 13, of which 6 were waited for; matrix products, arithmetic and copies ran while one was open for 2% of the time, Pallas kernels for 5%

profile of v5, /device:TPU:0, one launch (start us, length us, event | category | flops | bytes accessed | tf_op | source)
XLA Modules:
  0.0 300.2 jit_solution(13583627530887796732)
XLA Ops:
  0.0 1.2 dynamic_slice.65
  2.0 2.2 copy-done.3
  4.2 1.6 copy-done.9
  5.8 99.0 %spread.1 = (f32[4,2,128,1024]{3,2,1,0:T(8,128)S(1)}, f32[4,4,2,32,1024]{4,3,2,1,0:T(8,128)S(1)}, f32[2,1024,512]{2,1,0:T(8,128)S(1)}) custom-call(f32[1,2,2,256,1024]{4,3,2,1,0:T(8,128)S(1)} %copy-done.3, f32[2,256,1024]{2,1,0:T(8,128)S(1)} %copy-done.9, f32[2]{0:T(128)S(1)} %pad_maximum_fusion.1.scalars_ref), custom_call_target="tpu_custom_call" | custom-call | flops 100000000 | bytes 300000000 | tf_op jit(solution)/shard_map/spread/pallas_call | solution.py:416
  104.8 2.0 copy-done.2
  106.7 2.0 copy-done.5
  108.7 2.8 first.1
  111.6 28.0 %all_to_all.20.blocks_ref = f32[2,4,2,128,512]{4,3,2,1,0:T(8,128)S(1)} all-to-all(f32[2,4,2,128,512]{4,3,2,1,0:T(8,128)S(1)} %first.1), channel_id=1, replica_groups=mesh['shot'=2,'gy'=4,'freq'=2,'fld'=2] {'fld'}, dimensions={0} | all-to-all | bytes 8388608 | tf_op jit(solution)/shard_map/all_to_all | solution.py:548
  139.9 7.9 %middle.2 = f32[2,4,2,128,512]{4,3,2,1,0:T(8,128)S(1)} custom-call(f32[2,4,2,128,512]{4,3,2,1,0:T(8,128)S(1)} %all_to_all.20.blocks_ref, f32[2,1024,512]{2,1,0:T(8,128)} %copy-done.2, bf16[2,256,256]{2,1,0:T(8,128)(2,1)S(1)} %copy-done.7, bf16[2,256,256]{2,1,0:T(8,128)(2,1)S(1)} %copy-done.8, f32[2,8,128,256]{3,2,1,0:T(8,128)S(1)} %broadcast_in_dim.2.twiddle_ref), custom_call_target="tpu_custom_call" | custom-call | flops 3221225472 | bytes 12582912 | tf_op jit(solution)/shard_map/middle/pallas_call | solution.py:557
  147.8 1.9 copy-done.1
  149.8 5.6 %all-to-all-start.1 = ((f32[2,4,2,128,512]{4,3,2,1,0:T(8,128)}), f32[2,4,2,128,512]{4,3,2,1,0:T(8,128)}, u32[]{:S(2)}, u32[]{:S(2)}) async-start(f32[2,4,2,128,512]{4,3,2,1,0:T(8,128)} %copy-done.1), calls=%async_computation.1 | async-start | bytes 8388608 | tf_op jit(solution)/shard_map/all_to_all | solution.py:558
  155.4 4.5 %all-to-all-done.1.blocks_ref = f32[2,4,2,128,512]{4,3,2,1,0:T(8,128)} async-done(((f32[2,4,2,128,512]{4,3,2,1,0:T(8,128)}), f32[2,4,2,128,512]{4,3,2,1,0:T(8,128)}, u32[]{:S(2)}, u32[]{:S(2)}) %all-to-all-start.1) | async-done | bytes 4194336 | tf_op jit(solution)/shard_map/all_to_all | solution.py:558
  159.8 13.2 %last.2 = (f32[4,2,128,1024]{3,2,1,0:T(8,128)S(1)}, f32[2,4,2,128,512]{4,3,2,1,0:T(8,128)S(1)}) custom-call(f32[2,4,2,128,512]{4,3,2,1,0:T(8,128)} %all-to-all-done.1.blocks_ref, f32[4,4,2,32,1024]{4,3,2,1,0:T(8,128)} %copy-done.5, f32[2]{0:T(128)S(1)} %pad_maximum_fusion.1.scalars_ref, bf16[2,256,256]{2,1,0:T(8,128)(2,1)S(1)} %copy-done.7, ...), custom_call_target="tpu_custom_call" | custom-call | flops 3221225472 | bytes 12582912 | tf_op jit(solution)/shard_map/last/pallas_call | solution.py:562
  173.1 1.8 dynamic-slice_bitcast_fusion.3
  175.7 7.1 %all_to_all.21.blocks_ref = f32[2,4,2,128,512]{4,3,2,1,0:T(8,128)S(1)} all-to-all(f32[2,4,2,128,512]{4,3,2,1,0:T(8,128)S(1)} %get-tuple-element.17), channel_id=1, replica_groups=mesh['shot'=2,'gy'=4,'freq'=2,'fld'=2] {'fld'}, dimensions={0} | all-to-all | bytes 8388608 | tf_op jit(solution)/shard_map/all_to_all | solution.py:548
  182.8 7.9 %middle.3 = f32[2,4,2,128,512]{4,3,2,1,0:T(8,128)S(1)} custom-call(f32[2,4,2,128,512]{4,3,2,1,0:T(8,128)S(1)} %all_to_all.21.blocks_ref, f32[2,1024,512]{2,1,0:T(8,128)} %copy-done.2, bf16[2,256,256]{2,1,0:T(8,128)(2,1)S(1)} %copy-done.7, bf16[2,256,256]{2,1,0:T(8,128)(2,1)S(1)} %copy-done.8, f32[2,8,128,256]{3,2,1,0:T(8,128)S(1)} %broadcast_in_dim.2.twiddle_ref), custom_call_target="tpu_custom_call" | custom-call | flops 3221225472 | bytes 12582912 | tf_op jit(solution)/shard_map/middle/pallas_call | solution.py:557
  190.7 7.4 %all_to_all.22.blocks_ref = f32[2,4,2,128,512]{4,3,2,1,0:T(8,128)S(1)} all-to-all(f32[2,4,2,128,512]{4,3,2,1,0:T(8,128)S(1)} %middle.3), channel_id=1, replica_groups=mesh['shot'=2,'gy'=4,'freq'=2,'fld'=2] {'fld'}, dimensions={0} | all-to-all | bytes 8388608 | tf_op jit(solution)/shard_map/all_to_all | solution.py:558
  198.1 7.0 %last.3 = f32[4,2,128,1024]{3,2,1,0:T(8,128)S(1)} custom-call(f32[2,4,2,128,512]{4,3,2,1,0:T(8,128)S(1)} %all_to_all.22.blocks_ref, f32[4,4,2,32,1024]{4,3,2,1,0:T(8,128)S(1)} %copy-done.6, f32[2]{0:T(128)S(1)} %pad_maximum_fusion.1.scalars_ref, bf16[2,256,256]{2,1,0:T(8,128)(2,1)S(1)} %copy-done.7, bf16[2,256,256]{2,1,0:T(8,128)(2,1)S(1)} %copy-done.8, ...), custom_call_target="tpu_custom_call" | custom-call | flops 3221225472 | bytes 12582912 | tf_op jit(solution)/shard_map/last/pallas_call | solution.py:562
  205.1 2.0 copy-done
  207.3 1.3 collective-permute-start.7
  209.4 1.3 collective-permute-start.6
  210.6 1.8 fusion.2
  213.6 19.8 %collective-permute-done.7 = f32[2,128,1024]{2,1,0:T(8,128)} collective-permute-done((f32[2,128,1024]{2,1,0:T(8,128)S(1)}, f32[2,128,1024]{2,1,0:T(8,128)}, u32[]{:S(2)}, u32[]{:S(2)}) %collective-permute-start.7) | collective-permute-done | bytes 1048608 | tf_op jit(solution)/shard_map/ppermute | solution.py:585
  233.5 1.8 fusion
  235.3 1.2 collective-permute-start.8
  236.5 1.6 collective-permute-start.4
  238.1 23.4 %collective-permute-done = f32[2,128,1024]{2,1,0:T(8,128)} collective-permute-done((f32[2,128,1024]{2,1,0:T(8,128)}, f32[2,128,1024]{2,1,0:T(8,128)}, u32[]{:S(2)}, u32[]{:S(2)}) %collective-permute-start) | collective-permute-done | bytes 1048608 | tf_op jit(solution)/shard_map/ppermute | solution.py:585
  261.6 1.8 fusion.3
  264.9 23.9 %collective-permute-done.6 = f32[2,128,1024]{2,1,0:T(8,128)S(1)} collective-permute-done((f32[2,128,1024]{2,1,0:T(8,128)S(1)}, f32[2,128,1024]{2,1,0:T(8,128)S(1)}, u32[]{:S(2)}, u32[]{:S(2)}) %collective-permute-start.6) | collective-permute-done | bytes 1048608 | tf_op jit(solution)/shard_map/ppermute | solution.py:585
  288.8 1.4 fusion.1
  291.6 6.2 %collective-permute-done.9 = f32[128,512]{1,0:T(8,128)S(1)} collective-permute-done((f32[128,512]{1,0:T(8,128)S(1)}, f32[128,512]{1,0:T(8,128)S(1)}, u32[]{:S(2)}, u32[]{:S(2)}) %collective-permute-start.9) | collective-permute-done | bytes 262176 | tf_op jit(solution)/shard_map/ppermute | solution.py:591
  298.1 1.3 collective-permute-done.11
  (49 shorter events, 7.4 us)
Async XLA Ops:
  0.0 108.7 %copy-start.10 = (f32[2,8,128]{2,1,0:T(8,128)S(1)}, f32[2,8,128]{2,1,0:T(8,128)}, u32[]{:S(2)}) copy-start(f32[2,8,128]{2,1,0:T(8,128)} %constant.88.clone.twiddle_ref) | copy-start | bytes 24580
  2.0 2.2 copy-start.3
  4.2 1.6 copy-start.9
  5.8 102.9 %copy-start.7 = (bf16[2,256,256]{2,1,0:T(8,128)(2,1)S(1)}, bf16[2,256,256]{2,1,0:T(8,128)(2,1)}, u32[]{:S(2)}) copy-start(bf16[2,256,256]{2,1,0:T(8,128)(2,1)} %constant.86.clone.table_ref) | copy-start | bytes 786436
  104.8 2.0 copy-start.2
  106.7 2.0 copy-start.5
  111.6 28.3 %copy-start.8 = (bf16[2,256,256]{2,1,0:T(8,128)(2,1)S(1)}, bf16[2,256,256]{2,1,0:T(8,128)(2,1)}, u32[]{:S(2)}) copy-start(bf16[2,256,256]{2,1,0:T(8,128)(2,1)} %constant.87.clone.back_ref) | copy-start | bytes 786436
  147.8 1.9 copy-start.1
  149.8 10.1 %all-to-all-start.1 = ((f32[2,4,2,128,512]{4,3,2,1,0:T(8,128)}), f32[2,4,2,128,512]{4,3,2,1,0:T(8,128)}, u32[]{:S(2)}, u32[]{:S(2)}) async-start(f32[2,4,2,128,512]{4,3,2,1,0:T(8,128)} %copy-done.1), calls=%async_computation.1 | async-start | bytes 8388608 | tf_op jit(solution)/shard_map/all_to_all | solution.py:558
  173.1 2.6 copy-start.4
  174.9 35.7 %collective-permute-start.1 = (f32[2,128,1024]{2,1,0:T(8,128)}, f32[2,128,1024]{2,1,0:T(8,128)}, u32[]{:S(2)}, u32[]{:S(2)}) collective-permute-start(f32[2,128,1024]{2,1,0:T(8,128)} %get-tuple-element.20), channel_id=1, source_target_pairs={{0,4},{4,0},{8,12},{12,8},{1,5},{5,1},{9,13},{13,9},{2,6},{6,2},{1... | collective-permute-start | bytes 3145736 | tf_op jit(solution)/shard_map/ppermute | solution.py:585
  190.7 7.4 %copy-start.6 = (f32[4,4,2,32,1024]{4,3,2,1,0:T(8,128)S(1)}, f32[4,4,2,32,1024]{4,3,2,1,0:T(8,128)}, u32[]{:S(2)}) copy-start(f32[4,4,2,32,1024]{4,3,2,1,0:T(8,128)} %copy-done.5) | copy-start | bytes 12582916
  205.1 2.0 copy-start
  207.3 26.2 %collective-permute-start.7 = (f32[2,128,1024]{2,1,0:T(8,128)S(1)}, f32[2,128,1024]{2,1,0:T(8,128)}, u32[]{:S(2)}, u32[]{:S(2)}) collective-permute-start(f32[2,128,1024]{2,1,0:T(8,128)S(1)} %get-tuple-element.22), channel_id=1, source_target_pairs={{0,4},{4,0},{8,12},{12,8},{1,5},{5,1},{9,13},{13,9},{2,6},{6,2},{1... | collective-permute-start | bytes 3145736 | tf_op jit(solution)/shard_map/ppermute | solution.py:585
  208.6 53.0 %collective-permute-start = (f32[2,128,1024]{2,1,0:T(8,128)}, f32[2,128,1024]{2,1,0:T(8,128)}, u32[]{:S(2)}, u32[]{:S(2)}) collective-permute-start(f32[2,128,1024]{2,1,0:T(8,128)} %get-tuple-element.19), channel_id=1, source_target_pairs={{0,4},{4,0},{8,12},{12,8},{1,5},{5,1},{9,13},{13,9},{2,6},{6,2},{1... | collective-permute-start | bytes 3145736 | tf_op jit(solution)/shard_map/ppermute | solution.py:585
  209.4 79.4 %collective-permute-start.6 = (f32[2,128,1024]{2,1,0:T(8,128)S(1)}, f32[2,128,1024]{2,1,0:T(8,128)S(1)}, u32[]{:S(2)}, u32[]{:S(2)}) collective-permute-start(f32[2,128,1024]{2,1,0:T(8,128)S(1)} %get-tuple-element.21), channel_id=1, source_target_pairs={{0,4},{4,0},{8,12},{12,8},{1,5},{5,1},{9,13},{13,9},{2,6},{6,2},{1... | collective-permute-start | bytes 3145736 | tf_op jit(solution)/shard_map/ppermute | solution.py:585
  212.4 24.1 %collective-permute-start.2 = (f32[128,512]{1,0:T(8,128)S(1)}, f32[128,512]{1,0:T(8,128)S(1)}, u32[]{:S(2)}, u32[]{:S(2)}) collective-permute-start(f32[128,512]{1,0:T(8,128)S(1)} %constant_dynamic-slice_fusion.5), channel_id=1, source_target_pairs={{0,2},{2,0},{1,3},{3,1},{4,6},{6,4},{5,7},{7,5},{8,10},{10,8},{9,1... | collective-permute-start | bytes 786440 | tf_op jit(solution)/shard_map/ppermute | solution.py:591
  235.3 29.3 %collective-permute-start.8 = (f32[128,512]{1,0:T(8,128)S(1)}, f32[128,512]{1,0:T(8,128)S(1)}, u32[]{:S(2)}, u32[]{:S(2)}) collective-permute-start(f32[128,512]{1,0:T(8,128)S(1)} %constant_dynamic-slice_fusion.2), channel_id=1, source_target_pairs={{0,2},{2,0},{1,3},{3,1},{4,6},{6,4},{5,7},{7,5},{8,10},{10,8},{9,1... | collective-permute-start | bytes 786440 | tf_op jit(solution)/shard_map/ppermute | solution.py:591
  236.5 54.9 %collective-permute-start.4 = (f32[128,512]{1,0:T(8,128)S(1)}, f32[128,512]{1,0:T(8,128)S(1)}, u32[]{:S(2)}, u32[]{:S(2)}) collective-permute-start(f32[128,512]{1,0:T(8,128)S(1)} %dynamic-slice_add_fusion.1), channel_id=1, source_target_pairs={{0,8},{4,12},{8,0},{12,4},{1,9},{5,13},{9,1},{13,5},{2,10},{6,14},... | collective-permute-start | bytes 786440 | tf_op jit(solution)/shard_map/ppermute | solution.py:594
  263.3 28.1 %collective-permute-start.3 = (f32[128,512]{1,0:T(8,128)S(1)}, f32[128,512]{1,0:T(8,128)S(1)}, u32[]{:S(2)}, u32[]{:S(2)}) collective-permute-start(f32[128,512]{1,0:T(8,128)S(1)} %constant_dynamic-slice_fusion.4), channel_id=1, source_target_pairs={{0,2},{2,0},{1,3},{3,1},{4,6},{6,4},{5,7},{7,5},{8,10},{10,8},{9,1... | collective-permute-start | bytes 786440 | tf_op jit(solution)/shard_map/ppermute | solution.py:591
  264.6 33.2 %collective-permute-start.10 = (f32[128,512]{1,0:T(8,128)S(1)}, f32[128,512]{1,0:T(8,128)S(1)}, u32[]{:S(2)}, u32[]{:S(2)}) collective-permute-start(f32[128,512]{1,0:T(8,128)S(1)} %dynamic-slice_add_fusion), channel_id=1, source_target_pairs={{0,8},{4,12},{8,0},{12,4},{1,9},{5,13},{9,1},{13,5},{2,10},{6,14},... | collective-permute-start | bytes 786440 | tf_op jit(solution)/shard_map/ppermute | solution.py:594
  290.2 7.6 %collective-permute-start.9 = (f32[128,512]{1,0:T(8,128)S(1)}, f32[128,512]{1,0:T(8,128)S(1)}, u32[]{:S(2)}, u32[]{:S(2)}) collective-permute-start(f32[128,512]{1,0:T(8,128)S(1)} %constant_dynamic-slice_fusion.1), channel_id=1, source_target_pairs={{0,2},{2,0},{1,3},{3,1},{4,6},{6,4},{5,7},{7,5},{8,10},{10,8},{9,1... | collective-permute-start | bytes 786440 | tf_op jit(solution)/shard_map/ppermute | solution.py:591
  291.5 6.5 %collective-permute-start.5 = (f32[128,256]{1,0:T(8,128)S(1)}, f32[128,256]{1,0:T(8,128)S(1)}, u32[]{:S(2)}, u32[]{:S(2)}) collective-permute-start(f32[128,256]{1,0:T(8,128)S(1)} %constant_dynamic-slice_fusion.3), channel_id=1, source_target_pairs={{0,1},{1,0},{2,3},{3,2},{4,5},{5,4},{6,7},{7,6},{8,9},{9,8},{10,11... | collective-permute-start | bytes 393224 | tf_op jit(solution)/shard_map/ppermute | solution.py:600
  297.9 1.4 collective-permute-start.11
